TPU v7x, 32 devices: a whole 2x2x4 slice. The times are simulated.
32 devices in a mesh: grp: 2 (over x), seq: 8 (over z, y), head: 2 (over core).
Axes of the slice: x: 2, y: 2, z: 4, core: 2. Of those that a mesh axis runs over, the one named last changes fastest.
Arguments:
- query: bfloat16 [2048, 4096], P(('grp', 'seq'), 'head'), parts along dimension 0, may hold values from -6 to 6
- keys: bfloat16 [2048, 4096], P(('grp', 'seq'), 'head'), parts along dimension 0, may hold values from -6 to 6
- values: bfloat16 [2048, 4096], P(('grp', 'seq'), 'head'), parts along dimension 0, may hold values from -6 to 6
- resid: bfloat16 [2048, 3072], P(('grp', 'seq'), 'head'), parts along dimension 0, may hold values from -6 to 6
- attn_gain: float32 [4096], P('head'), may hold values from 0.2 to 1.8
- out_weight: bfloat16 [4096, 3072], P('head', 'seq'), may hold values from -0.09375 to 0.09375
- moe_gain: float32 [3072], replicated, may hold values from 0.2 to 1.8
- routes: int32 [2048, 2], P(('grp', 'seq')), parts along dimension 0, may hold values from 0 to 7, all different within a row; in each aligned block of 128 rows (0 to 127, 128 to 255, ...) at most 36 rows name the same one
- route_weights: float32 [2048, 2], P(('grp', 'seq')), parts along dimension 0, may hold values from 0.2 to 1
- w_gate: bfloat16 [3072, 36864], P(None, ('seq', 'head')), may hold values from -0.109375 to 0.109375
- w_up: bfloat16 [3072, 36864], P(None, ('seq', 'head')), may hold values from -0.109375 to 0.109375
- w_down: bfloat16 [36864, 3072], P(('seq', 'head')), may hold values from -0.09375 to 0.09375
Outputs:
- mixed: bfloat16 [2048, 3072], P(('grp', 'seq'), 'head'), parts along dimension 0
There are 2 independent parts, one for each index of `grp`. A program takes and returns all parts, laid end to end along the dimension named above; an argument that names none is the same for every part. Nothing has to cross between parts.
Inputs may be any that keep to these rules, and one draw needn't show every extreme that they name: A token's 2 experts differ. Within each aligned block of 128 tokens no expert is named by more than 36 routes, and in every draw some expert is named by exactly 36 routes of some block.
All inputs are finite; a program needn't handle non-finite values.
Results may differ from a plain program's by a relative error of at most 0.015.
Values may be sent and summed in bfloat16 or wider, within the bound.
A program may use at most 128 MiB of HBM per device.

v0:
```python
import jax
import jax.numpy as jnp
from jax import lax
from jax.sharding import PartitionSpec as P

D = 3072
HD = 128
EXPERTS = 8
TOP = 2
CAP = 36


EPS = 1e-06


def prefix(shard, axis, combine, identity):
    count, mine = (lax.axis_size(axis), lax.axis_index(axis))
    everything = lax.all_gather(shard.astype(jnp.bfloat16), axis)
    start = jnp.broadcast_to(jnp.asarray(identity, shard.dtype), shard.shape)

    def turn(k, before):
        reached = k < mine
        new = combine(before, everything[k].astype(shard.dtype))
        return jnp.where(reached, new, before)

    return lax.fori_loop(0, count, turn, start)


def accumulate_state_sums(earlier, later):
    return earlier + later


def per_device(
    query,
    keys,
    values,
    resid,
    attn_gain,
    out_weight,
    moe_gain,
    routes,
    route_weights,
    w_gate,
    w_up,
    w_down,
):
    tok_rows = query.shape[0]
    local_heads = query.shape[1] // HD
    seq_count = lax.axis_size("seq")
    head_count = lax.axis_size("head")
    head_pos = lax.axis_index("head")
    half_width = D // head_count
    slices = seq_count * head_count // EXPERTS
    q_three = query.reshape(tok_rows, local_heads, HD)
    k_three = keys.reshape(tok_rows, local_heads, HD)
    value_three_dims = values.reshape(tok_rows, local_heads, HD)
    block_own_state = jnp.einsum(
        "tnd,tne->nde", k_three, value_three_dims, preferred_element_type=jnp.float32
    )
    earlier = prefix(block_own_state, "seq", accumulate_state_sums, jnp.zeros_like(block_own_state))
    inter = jnp.einsum(
        "tnd,nde->tne", q_three, earlier.astype(jnp.bfloat16), preferred_element_type=jnp.float32
    )
    scores = jnp.einsum("tnd,snd->nts", q_three, k_three, preferred_element_type=jnp.float32)
    causal = jnp.arange(tok_rows)[:, None] >= jnp.arange(tok_rows)[None, :]
    resident_weight_parts = jnp.where(causal, scores, 0.0).astype(jnp.bfloat16)
    inside_block_scores = jnp.einsum(
        "rbj,jrh->brh", resident_weight_parts, value_three_dims, preferred_element_type=jnp.float32
    )
    attention = inter + inside_block_scores
    scale = lax.rsqrt(jnp.mean(attention * attention, axis=-1, keepdims=True) + EPS)
    normed = (
        (attention * scale * attn_gain.reshape(local_heads, HD))
        .astype(jnp.bfloat16)
        .reshape(tok_rows, local_heads * HD)
    )
    projected = jnp.dot(
        normed,
        lax.all_gather(out_weight, "seq", axis=1, tiled=True),
        preferred_element_type=jnp.float32,
    )
    placed = lax.dynamic_update_slice_in_dim(
        jnp.zeros((tok_rows, D), jnp.float32), resid.astype(jnp.float32), head_pos * half_width, 1
    )
    hidden = lax.psum((projected + placed).astype(jnp.bfloat16), "head")
    wide = hidden.astype(jnp.float32)
    moe_in = (
        wide * lax.rsqrt(jnp.mean(wide * wide, axis=-1, keepdims=True) + EPS) * moe_gain
    ).astype(jnp.bfloat16)
    own_rows = lax.dynamic_slice_in_dim(wide, head_pos * half_width, half_width, 1)
    flat_routes = routes.reshape(-1)
    onehot = (flat_routes[:, None] == jnp.arange(EXPERTS, dtype=jnp.int32)[None, :]).astype(
        jnp.int32
    )
    slots = jnp.sum((jnp.cumsum(onehot, axis=0) - 1) * onehot, axis=1)
    targets = (flat_routes * CAP + slots).reshape(tok_rows, TOP)
    slot_columns = jnp.arange(EXPERTS * CAP, dtype=jnp.int32)
    chosen = (targets[:, :, None] == slot_columns[None, None, :]).astype(jnp.float32)
    picker = jnp.sum(chosen, axis=1).astype(jnp.bfloat16)
    combine_weights = jnp.sum(chosen * route_weights[:, :, None], axis=1)
    contract_rows = (((0,), (0,)), ((), ()))
    own_half = lax.dynamic_slice_in_dim(moe_in, head_pos * half_width, half_width, 1)
    packed = lax.dot_general(
        picker, own_half, contract_rows, preferred_element_type=jnp.float32
    ).astype(jnp.bfloat16)
    copies = jnp.broadcast_to(
        packed.reshape(EXPERTS, 1, CAP, half_width), (EXPERTS, slices, CAP, half_width)
    ).reshape(EXPERTS * slices, CAP, half_width)
    received = lax.all_to_all(copies, ("seq", "head"), split_axis=0, concat_axis=2, tiled=True)
    count = received.shape[1]
    rows_in = received.reshape(count * seq_count, D)
    gate = jnp.dot(rows_in, w_gate, preferred_element_type=jnp.float32)
    upward = jnp.dot(rows_in, w_up, preferred_element_type=jnp.float32)
    inner = (jax.nn.silu(gate) * upward).astype(jnp.bfloat16)
    part = jnp.dot(inner, w_down, preferred_element_type=jnp.float32).astype(jnp.bfloat16)
    partial_value = part.reshape(count, seq_count * D)
    back = lax.all_to_all(partial_value, ("seq", "head"), split_axis=1, concat_axis=0, tiled=True)
    summed = jnp.sum(
        back.astype(jnp.float32).reshape(EXPERTS, slices, CAP, half_width), axis=1
    ).reshape(EXPERTS * CAP, half_width)
    moe_out = jnp.dot(combine_weights, summed, precision=lax.Precision.HIGHEST)
    return (own_rows + moe_out).astype(jnp.bfloat16)


def solution(mesh):
    return jax.shard_map(
        per_device,
        mesh=mesh,
        in_specs=(
            P(("grp", "seq"), "head"),
            P(("grp", "seq"), "head"),
            P(("grp", "seq"), "head"),
            P(("grp", "seq"), "head"),
            P("head"),
            P("head", "seq"),
            P(),
            P(("grp", "seq"), None),
            P(("grp", "seq"), None),
            P(None, ("seq", "head")),
            P(None, ("seq", "head")),
            P(("seq", "head"), None),
        ),
        out_specs=P(("grp", "seq"), "head"),
        check_vma=False,
    )
```

profile of v0, /device:TPU:0, one launch (start us, length us, event | category | flops | bytes accessed | tf_op | source)
XLA Modules:
  0.0 441.5 jit_solution(17192964790460254516)
XLA Ops:
  6.5 0.0 copy-start
  6.5 0.0 all-gather.6.cloned.1.call-start
  6.5 1.4 copy.79
  7.9 0.0 copy-start.7
  7.9 0.0 copy-start.6
  7.9 0.0 copy-done
  7.9 1.3 convolution_convert_fusion.2
  9.3 0.0 all-gather.6.cloned.1.call-update
  9.3 0.0 all-gather.4.cloned.1.call-start
  9.3 0.7 all-gather.4.cloned.1.call-update
  10.0 0.0 all-reduce.2.cloned.1.call-start
  10.1 0.0 copy-done.7
  10.1 0.1 copy.70
  10.2 0.1 eq.42
  10.4 0.1 eq.38
  10.5 0.0 copy-done.6
  10.5 0.1 dynamic-slice.1
  10.6 74.4 %all-gather.6.cloned.1.call-done = bf16[128,128,128]{2,1,0:T(8,128)(2,1)} async-done(((bf16[16,128,128]{2,1,0:T(8,128)(2,1)}), bf16[128,128,128]{2,1,0:T(8,128)(2,1)}) %all-gather.6.cloned.1.call-update) | async-done | bytes 4194320 | tf_op jit(solution)/shard_map/all_gather | solution.py:18
  85.0 13.3 %while.14 = (s32[]{:T(128)}, f32[16,128,128]{2,1,0:T(8,128)S(1)}, s32[]{:T(128)}, bf16[8,16,128,128]{3,2,1,0:T(8,128)(2,1)}, s32[]{:T(128)}, /*index=5*/s32[]{:T(128)}) while((s32[]{:T(128)}, f32[16,128,128]{2,1,0:T(8,128)S(1)}, s32[]{:T(128)}, bf16[8,16,128,128]{3,2,1,0:T(8,128)(2,1)}, s32[]{:T(128)}, /*index=5*/s32[]{:T(128)}) %tuple.43), condition=%wide.region_1.2_spmd.clone, body=%wide.region_0.1_spmd.clone.sunk | while | flops 1048580 | bytes 2621533 | solution.py:26
  85.0 1.6 add_select_fusion.2
  86.6 1.6 add_select_fusion.2
  88.3 1.6 add_select_fusion.2
  89.9 1.6 add_select_fusion.2
  91.6 1.7 add_select_fusion.2
  93.3 1.7 add_select_fusion.2
  95.0 1.7 add_select_fusion.2
  96.7 1.6 add_select_fusion.2
  98.3 1.6 convolution_bitcast_fusion.1
  99.9 1.9 multiply_reduce_fusion.1
  101.8 0.0 copy-done.5
  101.8 0.3 multiply_convert_fusion
  102.2 159.6 %all-gather.4.cloned.1.call-done = bf16[2048,3072]{1,0:T(8,128)(2,1)} async-done(((bf16[2048,384]{1,0:T(8,128)(2,1)}), bf16[2048,3072]{1,0:T(8,128)(2,1)}) %all-gather.4.cloned.1.call-update) | async-done | bytes 12582928 | tf_op jit(solution)/shard_map/all_gather | solution.py:79
  261.8 6.4 %fusion.31 = f32[128,3072]{1,0:T(8,128)S(1)} fusion(bf16[128,2048]{0,1:T(8,128)(2,1)S(1)} %bitcast.79, bf16[2048,3072]{1,0:T(8,128)(2,1)} %all-gather.4.cloned.1.call-done), kind=kOutput, calls=%fused_computation.49 | convolution fusion | flops 1610612736 | bytes 14680064 | tf_op jit(solution)/shard_map/dot_general | solution.py:77
  268.2 0.0 copy-done.4
  268.2 0.1 add_dynamic-update-slice_fusion
  268.4 0.0 copy-start.8
  268.4 1.0 convert_element_type.72
  269.4 0.0 all-reduce.2.cloned.1.call-update
  269.4 0.6 reduce-window.6
  270.0 0.2 slice_reduce_fusion
  270.3 0.1 fusion.22
  270.3 0.1 reduce_sum.58
  270.5 0.1 copy.72
  270.6 0.1 convert_reduce_fusion
  270.6 16.0 %all-reduce.2.cloned.1.call-done = bf16[128,3072]{1,0:T(8,128)(2,1)} async-done(((bf16[128,3072]{1,0:T(8,128)(2,1)}), bf16[128,3072]{1,0:T(8,128)(2,1)}) %all-reduce.2.cloned.1.call-update) | async-done | bytes 786448 | tf_op jit(solution)/shard_map/psum | solution.py:85
  286.7 1.4 multiply_reduce_fusion
  288.1 1.3 convert_element_type.73
  289.4 0.0 copy-start.2
  289.4 1.2 copy-done.2
  290.6 0.5 convolution_convert_fusion.1
  291.0 0.2 broadcast_in_dim.14
  291.2 0.2 broadcast_in_dim.15
  291.3 50.6 %all_to_all.28 = bf16[16,36,1536]{2,1,0:T(8,128)(2,1)S(1)} all-to-all(bf16[16,36,1536]{2,1,0:T(8,128)(2,1)S(1)} %bitcast.76), channel_id=1, replica_groups=mesh['grp'=2,'seq'=8,'head'=2] {'seq','head'}, dimensions={0} | all-to-all | bytes 3538944 | tf_op jit(solution)/shard_map/all_to_all | solution.py:109
  341.9 0.5 copy.73
  342.5 2.0 reshape.86
  344.5 11.5 %fusion.32 = f32[288,2304]{1,0:T(8,128)} fusion(bf16[288,3072]{1,0:T(8,128)(2,1)} %reshape.86, bf16[3072,2304]{1,0:T(8,128)(2,1)} %param.23), kind=kOutput, calls=%fused_computation.50 | convolution fusion | flops 4076863488 | bytes 18579456 | tf_op jit(solution)/shard_map/dot_general | solution.py:112
  356.0 20.3 %convolution_convert_fusion = bf16[288,3072]{1,0:T(8,128)(2,1)} fusion(bf16[2304,3072]{1,0:T(8,128)(2,1)} %param.25, bf16[288,3072]{1,0:T(8,128)(2,1)S(1)} %copy-done.3, bf16[3072,2304]{1,0:T(8,128)(2,1)} %param.24, f32[288,2304]{1,0:T(8,128)} %fusion.32), kind=kOutput, calls=%fused_computation.3 | convolution fusion | flops 8158593024 | bytes 34504704 | tf_op jit(solution)/shard_map/dot_general | solution.py:115
  376.2 2.8 all_to_all.24
  379.0 1.0 copy.74
  380.0 49.3 %all_to_all.29 = bf16[36,16,1536]{2,0,1:T(8,128)(2,1)S(1)} all-to-all(bf16[36,16,1536]{2,0,1:T(8,128)(2,1)S(1)} %copy.74), channel_id=1, replica_groups=mesh['grp'=2,'seq'=8,'head'=2] {'seq','head'}, dimensions={1} | all-to-all | bytes 3538944 | tf_op jit(solution)/shard_map/all_to_all | solution.py:117
  429.3 0.3 bitcast_reduce_fusion
  429.6 0.0 copy-start.1
  429.6 1.4 reshape.87
  431.0 3.9 fusion.1
  (14 shorter events, 0.1 us)
Async XLA Ops:
  6.5 1.4 copy-start
  6.5 78.5 %all-gather.6.cloned.1.call-start = ((), (), s32[]{:S(2)}) async-start(), calls=%async_computation.4 | async-start | bytes 4718592 | tf_op jit(solution)/shard_map/all_gather | solution.py:18
  7.9 2.2 copy-start.7
  7.9 2.6 copy-start.6
  9.3 252.5 %all-gather.4.cloned.1.call-start = ((), (), s32[]{:S(2)}) async-start(), calls=%async_computation.2 | async-start | bytes 14155776 | tf_op jit(solution)/shard_map/all_gather | solution.py:79
  10.0 276.7 %all-reduce.2.cloned.1.call-start = ((), (), s32[]{:S(2)}) async-start(), calls=%async_computation.3 | async-start | bytes 1572864 | tf_op jit(solution)/shard_map/psum | solution.py:85
  99.9 1.9 copy-start.5
  261.8 6.5 %copy-start.4 = (bf16[128,1536]{1,0:T(8,128)(2,1)S(1)}, bf16[128,1536]{1,0:T(8,128)(2,1)}, u32[]{:S(2)}) copy-start(bf16[128,1536]{1,0:T(8,128)(2,1)} %param.17) | copy-start | bytes 1179652
  268.4 2.2 copy-start.8
  289.4 1.2 copy-start.2
  344.5 11.5 %copy-start.3 = (bf16[288,3072]{1,0:T(8,128)(2,1)S(1)}, bf16[288,3072]{1,0:T(8,128)(2,1)}, u32[]{:S(2)}) copy-start(bf16[288,3072]{1,0:T(8,128)(2,1)} %reshape.86) | copy-start | bytes 5308420
  429.6 5.3 %copy-start.1 = (bf16[128,2048]{1,0:T(8,128)(2,1)S(1)}, bf16[128,2048]{1,0:T(8,128)(2,1)}, u32[]{:S(2)}) copy-start(bf16[128,2048]{1,0:T(8,128)(2,1)} %param.15) | copy-start | bytes 1572868
Sparse Core Ops, SparseCore 0:
  9.5 75.5 all-gather.5
  87.1 174.6 all-gather.3
  269.5 17.1 all-reduce.1
where the time goes:
time: 443 us; the launch traced here: 441 us
  waiting for transfers between devices  251 us (57%)
  blocking collectives  99.8 us (23%)
  matrix products  47.4 us (11%)
  other arithmetic  18.4 us (4%)
  between operations  13.4 us (3%)
  local copies, waits for them, and re-layouts  11.5 us (3%)
    all_gather x1, waiting for transfers between devices, per_device(): lax.all_gather(out_weight, 'seq', axis=1, tiled=True)  160 us
    all_gather x1, waiting for transfers between devices, prefix(): everything = lax.all_gather(shard.astype(jnp.bfloat16), axis)  74.4 us
    all_to_all x1, blocking collectives, per_device(): lax.all_to_all(copies, ('seq', 'head'), split_axis=0, concat_axis=2, tile...  50.6 us
    all_to_all x1, blocking collectives, per_device(): lax.all_to_all(partial_value, ('seq', 'head'), split_axis=1, concat_axis=...  49.3 us
    dot_general x1, matrix products, per_device(): jnp.dot(inner, w_down, preferred_element_type=jnp.float32)  20.3 us
    psum x1, waiting for transfers between devices, per_device(): hidden = lax.psum((projected + placed).astype(jnp.bfloat16), 'head')  16 us
    select_n x8, other arithmetic, turn(): return jnp.where(reached, new, before)  13.1 us
    dot_general x1, matrix products, per_device(): gate = jnp.dot(rows_in, w_gate, preferred_element_type=jnp.float32)  11.5 us
  transfers between devices with their start and end apart: 3, of which 3 were waited for; matrix products, arithmetic and copies ran while one was open for 4% of the time, Pallas kernels for 0%

commit v1 on v0

--- a/solution.py
+++ b/solution.py
@@ -13,21 +13,22 @@
 EPS = 1e-06
 
 
-def prefix(shard, axis, combine, identity):
-    count, mine = (lax.axis_size(axis), lax.axis_index(axis))
-    everything = lax.all_gather(shard.astype(jnp.bfloat16), axis)
-    start = jnp.broadcast_to(jnp.asarray(identity, shard.dtype), shard.shape)
-
-    def turn(k, before):
-        reached = k < mine
-        new = combine(before, everything[k].astype(shard.dtype))
-        return jnp.where(reached, new, before)
-
-    return lax.fori_loop(0, count, turn, start)
+def swap_heads(x):
+    pairs = [(i, lax.axis_size("head") - 1 - i) for i in range(lax.axis_size("head"))]
+    return lax.ppermute(x, "head", pairs)
 
 
-def accumulate_state_sums(earlier, later):
-    return earlier + later
+def earlier_sums(own):
+    count = lax.axis_size("seq")
+    blocks = lax.all_to_all(
+        own.reshape(count, own.shape[0] // count, own.shape[1]), "seq", 0, 0, tiled=True
+    )
+    running = jnp.zeros(blocks.shape[1:], jnp.float32)
+    before = []
+    for k in range(count):
+        before.append(running.astype(jnp.bfloat16))
+        running = running + blocks[k].astype(jnp.float32)
+    return lax.all_to_all(jnp.stack(before), "seq", 0, 0, tiled=True).reshape(own.shape)
 
 
 def per_device(
@@ -57,10 +58,10 @@
     block_own_state = jnp.einsum(
         "tnd,tne->nde", k_three, value_three_dims, preferred_element_type=jnp.float32
     )
-    earlier = prefix(block_own_state, "seq", accumulate_state_sums, jnp.zeros_like(block_own_state))
-    inter = jnp.einsum(
-        "tnd,nde->tne", q_three, earlier.astype(jnp.bfloat16), preferred_element_type=jnp.float32
-    )
+    earlier = earlier_sums(
+        block_own_state.astype(jnp.bfloat16).reshape(local_heads * HD, HD)
+    ).reshape(local_heads, HD, HD)
+    inter = jnp.einsum("tnd,nde->tne", q_three, earlier, preferred_element_type=jnp.float32)
     scores = jnp.einsum("tnd,snd->nts", q_three, k_three, preferred_element_type=jnp.float32)
     causal = jnp.arange(tok_rows)[:, None] >= jnp.arange(tok_rows)[None, :]
     resident_weight_parts = jnp.where(causal, scores, 0.0).astype(jnp.bfloat16)
@@ -74,15 +75,28 @@
         .astype(jnp.bfloat16)
         .reshape(tok_rows, local_heads * HD)
     )
-    projected = jnp.dot(
-        normed,
-        lax.all_gather(out_weight, "seq", axis=1, tiled=True),
-        preferred_element_type=jnp.float32,
+    everyone = lax.all_gather(normed, "seq", axis=0, tiled=True)
+    columns = out_weight.shape[1] // head_count
+    projected = jnp.dot(everyone, out_weight, preferred_element_type=jnp.float32)
+    kept = lax.dynamic_slice_in_dim(projected, head_pos * columns, columns, 1)
+    passed = lax.dynamic_slice_in_dim(projected, (1 - head_pos) * columns, columns, 1)
+    mine = (kept + swap_heads(passed.astype(jnp.bfloat16)).astype(jnp.float32)).astype(jnp.bfloat16)
+    mine = lax.all_to_all(
+        mine.reshape(seq_count, tok_rows, columns), "seq", 0, 0, tiled=True
     )
-    placed = lax.dynamic_update_slice_in_dim(
-        jnp.zeros((tok_rows, D), jnp.float32), resid.astype(jnp.float32), head_pos * half_width, 1
+    other = swap_heads(mine)
+    first = jnp.where(head_pos == 0, mine, other)
+    second = jnp.where(head_pos == 0, other, mine)
+    attended = jnp.stack([first, second], 1).transpose(2, 0, 1, 3).reshape(tok_rows, D)
+    resid_other = swap_heads(resid)
+    resid_all = jnp.concatenate(
+        [
+            jnp.where(head_pos == 0, resid, resid_other),
+            jnp.where(head_pos == 0, resid_other, resid),
+        ],
+        axis=1,
     )
-    hidden = lax.psum((projected + placed).astype(jnp.bfloat16), "head")
+    hidden = (attended.astype(jnp.float32) + resid_all.astype(jnp.float32)).astype(jnp.bfloat16)
     wide = hidden.astype(jnp.float32)
     moe_in = (
         wide * lax.rsqrt(jnp.mean(wide * wide, axis=-1, keepdims=True) + EPS) * moe_gain
@@ -103,22 +117,36 @@
     packed = lax.dot_general(
         picker, own_half, contract_rows, preferred_element_type=jnp.float32
     ).astype(jnp.bfloat16)
+    chips = slices // head_count
     copies = jnp.broadcast_to(
-        packed.reshape(EXPERTS, 1, CAP, half_width), (EXPERTS, slices, CAP, half_width)
-    ).reshape(EXPERTS * slices, CAP, half_width)
-    received = lax.all_to_all(copies, ("seq", "head"), split_axis=0, concat_axis=2, tiled=True)
-    count = received.shape[1]
-    rows_in = received.reshape(count * seq_count, D)
+        packed.reshape(EXPERTS, 1, CAP, half_width), (EXPERTS, chips, CAP, half_width)
+    ).reshape(EXPERTS * chips, CAP, half_width)
+    received = lax.all_to_all(copies, "seq", 0, 0, tiled=True).reshape(-1, half_width)
+    partner = swap_heads(received)
+    rows_in = jnp.concatenate(
+        [
+            jnp.where(head_pos == 0, received, partner),
+            jnp.where(head_pos == 0, partner, received),
+        ],
+        axis=1,
+    )
     gate = jnp.dot(rows_in, w_gate, preferred_element_type=jnp.float32)
     upward = jnp.dot(rows_in, w_up, preferred_element_type=jnp.float32)
     inner = (jax.nn.silu(gate) * upward).astype(jnp.bfloat16)
     part = jnp.dot(inner, w_down, preferred_element_type=jnp.float32).astype(jnp.bfloat16)
-    partial_value = part.reshape(count, seq_count * D)
-    back = lax.all_to_all(partial_value, ("seq", "head"), split_axis=1, concat_axis=0, tiled=True)
-    summed = jnp.sum(
-        back.astype(jnp.float32).reshape(EXPERTS, slices, CAP, half_width), axis=1
-    ).reshape(EXPERTS * CAP, half_width)
-    moe_out = jnp.dot(combine_weights, summed, precision=lax.Precision.HIGHEST)
+    kept = lax.dynamic_slice_in_dim(part, head_pos * half_width, half_width, 1)
+    passed = lax.dynamic_slice_in_dim(part, (1 - head_pos) * half_width, half_width, 1)
+    total = (kept.astype(jnp.float32) + swap_heads(passed).astype(jnp.float32)).astype(jnp.bfloat16)
+    back = lax.all_to_all(
+        total.reshape(seq_count, CAP, half_width), "seq", 0, 0, tiled=True
+    ).reshape(EXPERTS, chips, CAP, half_width)
+    high = combine_weights.astype(jnp.bfloat16)
+    low = (combine_weights - high.astype(jnp.float32)).astype(jnp.bfloat16)
+    moe_out = jnp.zeros((tok_rows, half_width), jnp.float32)
+    for chip in range(chips):
+        piece = back[:, chip].reshape(EXPERTS * CAP, half_width)
+        moe_out = moe_out + jnp.dot(high, piece, preferred_element_type=jnp.float32)
+        moe_out = moe_out + jnp.dot(low, piece, preferred_element_type=jnp.float32)
     return (own_rows + moe_out).astype(jnp.bfloat16)
 
 

time: 443 us -> 258 us (0.58)
  waiting for transfers between devices: 251 us -> 119 us
  blocking collectives: 99.8 us -> 56.2 us
  starting transfers between devices: 0.08 us -> 15.2 us
  matrix products: 47.4 us -> 35.7 us
  other arithmetic: 18.4 us -> 9.55 us
    all_gather x2 -> x1, waiting for transfers between devices: 234 us -> 73.8 us  [per_device(): everyone = lax.all_gather(normed, 'seq', axis=0, tiled=True)]
    all_to_all x2, blocking collectives: 99.8 us -> 56.2 us  [the longest x1 28.1 us: per_device(): lax.all_to_all(copies, 'seq', 0, 0, tiled=True).reshape(-1, half_width)]
    all_to_all x0 -> x3, waiting for transfers between devices: none -> 37.9 us  [the longest x1 14.6 us: earlier_sums(): lax.all_to_all(jnp.stack(before), 'seq', 0, 0, tiled=True)]
    psum x1 -> x0, waiting for transfers between devices: 16 us -> none  [per_device(): hidden = lax.psum((projected + placed).astype(jnp.bfloat16), 'head')]
    all_to_all x0 -> x3, starting transfers between devices: none -> 14.4 us  [the longest x1 7.31 us: earlier_sums(): lax.all_to_all(own.reshape(count, own.shape[0] // count, own.shape[1]), '...]
    dot_general x1, matrix products: 20.3 us -> 7.13 us  [per_device(): jnp.dot(inner, w_down, preferred_element_type=jnp.float32)]
    select_n x8 -> x2, other arithmetic: 13.1 us -> 0.18 us  [the longest x1 0.12 us: per_device(): jnp.where(head_pos == 0, received, partner)]
    ppermute x0 -> x5, waiting for transfers between devices: none -> 6.9 us  [swap_heads(): return lax.ppermute(x, 'head', pairs)]
  transfers between devices with their start and end apart: 3 -> 9, of which waited for: 3 -> 8; matrix products, arithmetic and copies ran while one was open for 4% -> 2% of each run, Pallas kernels for 0% -> 0%
where the time goes in v1:
time: 258 us; the launch traced here: 257 us
  waiting for transfers between devices  119 us (46%)
  blocking collectives  56.2 us (22%)
  matrix products  35.7 us (14%)
  starting transfers between devices  15.2 us (6%)
  between operations  13.8 us (5%)
  other arithmetic  9.55 us (4%)
  local copies, waits for them, and re-layouts  8.02 us (3%)
    all_gather x1, waiting for transfers between devices, per_device(): everyone = lax.all_gather(normed, 'seq', axis=0, tiled=True)  73.8 us
    all_to_all x1, blocking collectives, per_device(): lax.all_to_all(copies, 'seq', 0, 0, tiled=True).reshape(-1, half_width)  28.1 us
    all_to_all x1, blocking collectives, per_device(): lax.all_to_all(total.reshape(seq_count, CAP, half_width), 'seq', 0, 0, ti...  28.1 us
    all_to_all x1, waiting for transfers between devices, earlier_sums(): lax.all_to_all(jnp.stack(before), 'seq', 0, 0, tiled=True)  14.6 us
    all_to_all x1, waiting for transfers between devices, earlier_sums(): lax.all_to_all(own.reshape(count, own.shape[0] // count, own.shape[1]), '...  13.9 us
    all_to_all x1, waiting for transfers between devices, per_device(): lax.all_to_all(mine.reshape(seq_count, tok_rows, columns), 'seq', 0, 0, t...  9.47 us
    dot_general x1, matrix products, per_device(): upward = jnp.dot(rows_in, w_up, preferred_element_type=jnp.float32)  9.36 us
    all_to_all x1, starting transfers between devices, earlier_sums(): lax.all_to_all(own.reshape(count, own.shape[0] // count, own.shape[1]), '...  7.31 us
  transfers between devices with their start and end apart: 9, of which 8 were waited for; matrix products, arithmetic and copies ran while one was open for 2% of the time, Pallas kernels for 0%

profile of v1, /device:TPU:0, one launch (start us, length us, event | category | flops | bytes accessed | tf_op | source)
XLA Modules:
  0.0 257.2 jit_solution(11705211978842779288)
XLA Ops:
  6.5 1.4 copy.70
  8.0 2.4 convolution_convert_fusion.2
  10.3 7.3 %all-to-all-start = ((bf16[8,256,128]{2,1,0:T(8,128)(2,1)}), bf16[8,256,128]{2,1,0:T(8,128)(2,1)S(1)}, u32[]{:S(2)}, u32[]{:S(2)}) async-start(bf16[8,256,128]{2,1,0:T(8,128)(2,1)} %bitcast), calls=%async_computation | async-start | bytes 1048576 | tf_op jit(solution)/shard_map/all_to_all | solution.py:23
  17.7 0.6 broadcast_dynamic-update-slice_fusion
  18.3 13.9 %all-to-all-done = bf16[8,256,128]{2,1,0:T(8,128)(2,1)S(1)} async-done(((bf16[8,256,128]{2,1,0:T(8,128)(2,1)}), bf16[8,256,128]{2,1,0:T(8,128)(2,1)S(1)}, u32[]{:S(2)}, u32[]{:S(2)}) %all-to-all-start) | async-done | bytes 524320 | tf_op jit(solution)/shard_map/all_to_all | solution.py:23
  32.1 0.6 slice_dynamic-update-slice_fusion
  32.8 0.6 fusion.32
  33.4 0.6 convert_dynamic-update-slice_fusion.1
  34.0 0.7 fusion.31
  34.7 0.7 convert_dynamic-update-slice_fusion
  35.4 0.6 fusion.30
  36.0 0.7 fusion.33
  36.7 3.6 %all-to-all-start.1 = ((bf16[8,256,128]{2,1,0:T(8,128)(2,1)}), bf16[8,256,128]{2,1,0:T(8,128)(2,1)S(1)}, u32[]{:S(2)}, u32[]{:S(2)}) async-start(bf16[8,256,128]{2,1,0:T(8,128)(2,1)} %fusion.33), calls=%async_computation.1 | async-start | bytes 1048576 | tf_op jit(solution)/shard_map/all_to_all | solution.py:31
  40.4 14.6 %all-to-all-done.1 = bf16[8,256,128]{2,1,0:T(8,128)(2,1)S(1)} async-done(((bf16[8,256,128]{2,1,0:T(8,128)(2,1)}), bf16[8,256,128]{2,1,0:T(8,128)(2,1)S(1)}, u32[]{:S(2)}, u32[]{:S(2)}) %all-to-all-start.1) | async-done | bytes 524320 | tf_op jit(solution)/shard_map/all_to_all | solution.py:31
  55.0 1.5 convolution_bitcast_fusion.1
  56.5 2.4 multiply_reduce_fusion.1
  58.9 1.1 multiply_convert_fusion.2
  60.1 73.8 %all-gather.2.cloned.1.call-done = bf16[1024,2048]{0,1:T(8,128)(2,1)} async-done(((bf16[128,2048]{0,1:T(8,128)(2,1)}), bf16[1024,2048]{0,1:T(8,128)(2,1)}) %all-gather.2.cloned.1.call-update) | async-done | bytes 4194320 | tf_op jit(solution)/shard_map/all_gather | solution.py:78
  133.9 4.0 %fusion.48 = f32[1024,384]{0,1:T(8,128)S(1)} fusion(bf16[1024,2048]{0,1:T(8,128)(2,1)} %all-gather.2.cloned.1.call-done, bf16[2048,384]{1,0:T(8,128)(2,1)S(1)} %copy-done), kind=kOutput, calls=%fused_computation.89 | convolution fusion | flops 1610612736 | bytes 7340032 | tf_op jit(solution)/shard_map/dot_general | solution.py:80
  138.0 0.8 dynamic-slice_convert_fusion
  138.8 0.5 collective-permute-start.2
  139.3 0.1 copy.64
  139.4 0.1 eq.51
  139.6 0.1 eq.47
  139.7 1.0 collective-permute-done
  140.7 0.8 copy_bitcast_fusion
  141.5 3.5 %all-to-all-start.2 = ((bf16[8,128,192]{1,2,0:T(8,128)(2,1)}), bf16[8,128,192]{1,2,0:T(8,128)(2,1)S(1)}, u32[]{:S(2)}, u32[]{:S(2)}) async-start(bf16[8,128,192]{1,2,0:T(8,128)(2,1)} %copy_bitcast_fusion), calls=%async_computation.2 | async-start | bytes 786432 | tf_op jit(solution)/shard_map/all_to_all | solution.py:84
  145.0 0.6 reduce-window.6
  145.6 0.2 slice_reduce_fusion
  145.9 0.1 fusion.37
  146.0 0.1 reduce_sum.49
  146.1 0.1 copy.66
  146.2 0.8 dynamic-slice
  147.0 0.7 select_reduce_fusion
  147.7 9.5 %all-to-all-done.2 = bf16[8,128,192]{1,2,0:T(8,128)(2,1)S(1)} async-done(((bf16[8,128,192]{1,2,0:T(8,128)(2,1)}), bf16[8,128,192]{1,2,0:T(8,128)(2,1)S(1)}, u32[]{:S(2)}, u32[]{:S(2)}) %all-to-all-start.2) | async-done | bytes 393248 | tf_op jit(solution)/shard_map/all_to_all | solution.py:84
  157.2 0.1 broadcast_select_fusion.3
  157.3 0.2 copy.67
  157.5 0.2 copy.68
  157.7 1.2 collective-permute-done.1
  158.9 0.1 select_bitcast_fusion.1
  159.0 0.1 maximum_convert_fusion
  159.1 0.4 multiply_reduce_fusion
  159.5 0.5 copy.63
  160.0 1.2 fusion.8
  161.2 1.2 copy-done.2
  162.4 0.5 convolution_convert_fusion.1
  162.8 0.2 reshape_reshape.11
  163.0 28.1 %all_to_all.25 = bf16[8,36,1536]{2,1,0:T(8,128)(2,1)S(1)} all-to-all(bf16[8,36,1536]{2,1,0:T(8,128)(2,1)S(1)} %reshape_reshape.11), channel_id=1, replica_groups=mesh['grp'=2,'seq'=8,'head'=2] {'seq'}, dimensions={0} | all-to-all | bytes 1769472 | tf_op jit(solution)/shard_map/all_to_all | solution.py:124
  191.2 0.2 reshape.78
  191.3 0.1 collective-permute-start.3
  191.4 2.4 collective-permute-done.3
  193.8 0.1 broadcast_select_fusion.1
  194.0 9.4 %fusion.6 = f32[288,2304]{1,0:T(8,128)} fusion(bf16[3072,2304]{1,0:T(8,128)(2,1)} %param.22, bf16[288,1536]{1,0:T(8,128)(2,1)S(1)} %get-tuple-element.10, bf16[288,1536]{1,0:T(8,128)(2,1)S(1)} %get-tuple-element.9), kind=kOutput, calls=%fused_computation.19 | convolution fusion | flops 4080402432 | bytes 18579456 | tf_op jit(solution)/shard_map/dot_general | solution.py:134
  203.4 5.8 %fusion.7 = f32[288,2304]{1,0:T(8,128)} fusion(bf16[3072,2304]{1,0:T(8,128)(2,1)S(1)} %bitcast.90, bf16[288,1536]{1,0:T(8,128)(2,1)S(1)} %get-tuple-element.10, bf16[288,1536]{1,0:T(8,128)(2,1)S(1)} %get-tuple-element.9), kind=kOutput, calls=%fused_computation.20 | convolution fusion | flops 4080402432 | bytes 18579456 | tf_op jit(solution)/shard_map/dot_general | solution.py:133
  209.3 7.1 %convolution_convert_fusion = bf16[288,3072]{1,0:T(8,128)(2,1)S(1)} fusion(bf16[2304,3072]{1,0:T(8,128)(2,1)S(1)} %bitcast.92, f32[288,2304]{1,0:T(8,128)} %fusion.6, f32[288,2304]{1,0:T(8,128)} %fusion.7), kind=kOutput, calls=%fused_computation | convolution fusion | flops 4081729536 | bytes 21233664 | tf_op jit(solution)/shard_map/dot_general | solution.py:136
  216.4 0.1 constant_dynamic-slice_fusion
  216.5 0.2 collective-permute-start.4
  216.7 2.3 collective-permute-done.4
  219.0 0.3 add_convert_fusion
  219.2 0.2 reshape.79
  219.4 28.1 %all_to_all.26 = bf16[8,36,1536]{2,1,0:T(8,128)(2,1)S(1)} all-to-all(bf16[8,36,1536]{2,1,0:T(8,128)(2,1)S(1)} %reshape.79), channel_id=1, replica_groups=mesh['grp'=2,'seq'=8,'head'=2] {'seq'}, dimensions={0} | all-to-all | bytes 1769472 | tf_op jit(solution)/shard_map/all_to_all | solution.py:140
  247.5 0.2 reshape_squeeze_reshape.3
  247.7 1.4 fusion.35
  249.2 1.2 fusion.1
  (55 shorter events, 0.3 us)
Async XLA Ops:
  6.5 127.4 %copy-start = (bf16[2048,384]{1,0:T(8,128)(2,1)S(1)}, bf16[2048,384]{1,0:T(8,128)(2,1)}, u32[]{:S(2)}) copy-start(bf16[2048,384]{1,0:T(8,128)(2,1)} %param.17) | copy-start | bytes 4718596
  10.3 21.8 %all-to-all-start = ((bf16[8,256,128]{2,1,0:T(8,128)(2,1)}), bf16[8,256,128]{2,1,0:T(8,128)(2,1)S(1)}, u32[]{:S(2)}, u32[]{:S(2)}) async-start(bf16[8,256,128]{2,1,0:T(8,128)(2,1)} %bitcast), calls=%async_computation | async-start | bytes 1048576 | tf_op jit(solution)/shard_map/all_to_all | solution.py:23
  17.6 37.3 %copy-start.5 = (bf16[128,2048]{1,0:T(8,128)(2,1)S(1)}, bf16[128,2048]{1,0:T(8,128)(2,1)}, u32[]{:S(2)}) copy-start(bf16[128,2048]{1,0:T(8,128)(2,1)} %param.12) | copy-start | bytes 1572868
  36.7 18.3 %all-to-all-start.1 = ((bf16[8,256,128]{2,1,0:T(8,128)(2,1)}), bf16[8,256,128]{2,1,0:T(8,128)(2,1)S(1)}, u32[]{:S(2)}, u32[]{:S(2)}) async-start(bf16[8,256,128]{2,1,0:T(8,128)(2,1)} %fusion.33), calls=%async_computation.1 | async-start | bytes 1048576 | tf_op jit(solution)/shard_map/all_to_all | solution.py:31
  40.3 93.6 %all-gather.2.cloned.1.call-start = ((), (), s32[]{:S(2)}) async-start(), calls=%async_computation.5 | async-start | bytes 4718592 | tf_op jit(solution)/shard_map/all_gather | solution.py:78
  56.5 2.4 copy-start.10
  60.1 78.7 %copy-start.7 = (bf16[128,1536]{1,0:T(8,128)(2,1)S(1)}, bf16[128,1536]{1,0:T(8,128)(2,1)}, u32[]{:S(2)}) copy-start(bf16[128,1536]{1,0:T(8,128)(2,1)} %param.15) | copy-start | bytes 1179652
  60.1 79.2 %copy-start.11 = (s32[128,2]{0,1:T(2,128)S(1)}, s32[128,2]{0,1:T(2,128)}, u32[]{:S(2)}) copy-start(s32[128,2]{0,1:T(2,128)} %param.19) | copy-start | bytes 3076
  138.0 9.0 %copy-start.12 = (f32[128,2]{0,1:T(2,128)S(1)}, f32[128,2]{0,1:T(2,128)}, u32[]{:S(2)}) copy-start(f32[128,2]{0,1:T(2,128)} %param.20) | copy-start | bytes 3076
  138.0 19.2 %copy-start.8 = (bf16[128,1536]{1,0:T(8,128)(2,1)S(1)}, bf16[128,1536]{1,0:T(8,128)(2,1)}, u32[]{:S(2)}) copy-start(bf16[128,1536]{1,0:T(8,128)(2,1)} %param.15) | copy-start | bytes 1179652
  138.8 1.9 collective-permute-start
  138.8 18.4 %collective-permute-start.2 = (bf16[128,1536]{1,0:T(8,128)(2,1)S(1)}, bf16[128,1536]{1,0:T(8,128)(2,1)S(1)}, u32[]{:S(2)}, u32[]{:S(2)}) collective-permute-start(bf16[128,1536]{1,0:T(8,128)(2,1)S(1)} %copy-done.7), channel_id=1, source_target_pairs={{0,1},{1,0},{2,3},{3,2},{4,5},{5,4},{6,7},{7,6},{8,9},{9,8},{10,11... | collective-permute-start | bytes 1179656 | tf_op jit(solution)/shard_map/ppermute | solution.py:18
  141.5 15.6 %all-to-all-start.2 = ((bf16[8,128,192]{1,2,0:T(8,128)(2,1)}), bf16[8,128,192]{1,2,0:T(8,128)(2,1)S(1)}, u32[]{:S(2)}, u32[]{:S(2)}) async-start(bf16[8,128,192]{1,2,0:T(8,128)(2,1)} %copy_bitcast_fusion), calls=%async_computation.2 | async-start | bytes 786432 | tf_op jit(solution)/shard_map/all_to_all | solution.py:84
  157.2 1.7 collective-permute-start.1
  157.3 1.7 copy-start.4
  160.0 2.4 copy-start.9
  161.2 1.2 copy-start.2
  191.3 2.5 collective-permute-start.3
  193.8 9.6 %slice-start = ((s8[14155776]{0:T(1024)(128)(4,1)}), s8[4194304]{0:T(1024)(128)(4,1)S(1)}, s32[]{:S(2)}) async-start(s8[14155776]{0:T(1024)(128)(4,1)} %bitcast.89), calls=%async_computation.6 | async-start | bytes 8388608
  194.0 9.4 %slice-start.1 = ((s8[14155776]{0:T(1024)(128)(4,1)}), s8[4194304]{0:T(1024)(128)(4,1)S(1)}, s32[]{:S(2)}) async-start(s8[14155776]{0:T(1024)(128)(4,1)} %bitcast.89), calls=%async_computation.7 | async-start | bytes 8388608
  194.0 9.4 %slice-start.2 = ((s8[14155776]{0:T(1024)(128)(4,1)}), s8[4194304]{0:T(1024)(128)(4,1)S(1)}, s32[]{:S(2)}) async-start(s8[14155776]{0:T(1024)(128)(4,1)} %bitcast.89), calls=%async_computation.8 | async-start | bytes 8388608
  194.0 9.4 %slice-start.3 = ((s8[14155776]{0:T(1024)(128)(4,1)}), s8[1572864]{0:T(1024)(128)(4,1)S(1)}, s32[]{:S(2)}) async-start(s8[14155776]{0:T(1024)(128)(4,1)} %bitcast.89), calls=%async_computation.9 | async-start | bytes 3145728
  194.0 15.3 %slice-start.4 = ((s8[14155776]{0:T(1024)(128)(4,1)}), s8[4194304]{0:T(1024)(128)(4,1)S(1)}, s32[]{:S(2)}) async-start(s8[14155776]{0:T(1024)(128)(4,1)} %bitcast.91), calls=%async_computation.10 | async-start | bytes 8388608
  194.0 15.2 %slice-start.5 = ((s8[14155776]{0:T(1024)(128)(4,1)}), s8[4194304]{0:T(1024)(128)(4,1)S(1)}, s32[]{:S(2)}) async-start(s8[14155776]{0:T(1024)(128)(4,1)} %bitcast.91), calls=%async_computation.11 | async-start | bytes 8388608
  194.0 15.2 %slice-start.6 = ((s8[14155776]{0:T(1024)(128)(4,1)}), s8[4194304]{0:T(1024)(128)(4,1)S(1)}, s32[]{:S(2)}) async-start(s8[14155776]{0:T(1024)(128)(4,1)} %bitcast.91), calls=%async_computation.12 | async-start | bytes 8388608
  203.4 5.8 %slice-start.7 = ((s8[14155776]{0:T(1024)(128)(4,1)}), s8[1572864]{0:T(1024)(128)(4,1)S(1)}, s32[]{:S(2)}) async-start(s8[14155776]{0:T(1024)(128)(4,1)} %bitcast.91), calls=%async_computation.13 | async-start | bytes 3145728
  216.5 2.5 collective-permute-start.4
  247.7 1.5 copy-start.3
  247.7 1.5 copy-start.6
  247.7 2.6 %copy-start.1 = (bf16[2048,384]{1,0:T(8,128)(2,1)S(1)}, bf16[2048,384]{1,0:T(8,128)(2,1)}, u32[]{:S(2)}) copy-start(bf16[2048,384]{1,0:T(8,128)(2,1)} %param.17) | copy-start | bytes 4718596
Sparse Core Ops, SparseCore 0:
  60.2 73.6 all-gather.1

commit v2 on v1

--- a/solution.py
+++ b/solution.py
@@ -1,6 +1,10 @@
+import functools
+
 import jax
 import jax.numpy as jnp
 from jax import lax
+from jax.experimental import pallas as pl
+from jax.experimental.pallas import tpu as pltpu
 from jax.sharding import PartitionSpec as P
 
 D = 3072
@@ -29,6 +33,175 @@
         before.append(running.astype(jnp.bfloat16))
         running = running + blocks[k].astype(jnp.float32)
     return lax.all_to_all(jnp.stack(before), "seq", 0, 0, tiled=True).reshape(own.shape)
+
+
+def greet_all(me, count):
+    barrier = pltpu.get_barrier_semaphore()
+
+    def greet(step, carry):
+        pl.semaphore_signal(
+            barrier,
+            inc=1,
+            device_id={"seq": lax.rem(me + step, count)},
+            device_id_type=pl.DeviceIdType.MESH,
+        )
+        return carry
+
+    lax.fori_loop(1, count, greet, 0)
+    pl.semaphore_wait(barrier, count - 1)
+
+
+def project_kernel(
+    count, shard_ref, weight_ref, back_ref, held, made, send_sem, recv_sem, back_send, back_recv, own_sem
+):
+    me = lax.axis_index("seq")
+    outer, inner = me // 2, lax.rem(me, 2)
+    outers = count // 2
+    partner = outer * 2 + (1 - inner)
+    greet_all(me, count)
+
+    def pass_on(source, src, way, to):
+        return pltpu.make_async_remote_copy(
+            src_ref=src,
+            dst_ref=held.at[source],
+            send_sem=send_sem.at[source, way],
+            recv_sem=recv_sem.at[source],
+            device_id={"seq": to},
+            device_id_type=pl.DeviceIdType.MESH,
+        )
+
+    def go_home(source):
+        return pltpu.make_async_remote_copy(
+            src_ref=made.at[source],
+            dst_ref=back_ref.at[me],
+            send_sem=back_send.at[source],
+            recv_sem=back_recv.at[me],
+            device_id={"seq": source},
+            device_id_type=pl.DeviceIdType.MESH,
+        )
+
+    def multiply(source, block):
+        made[source] = jnp.dot(
+            block[...], weight_ref[...], preferred_element_type=jnp.float32
+        ).astype(jnp.bfloat16)
+
+    @pl.when(outer + 1 < outers)
+    def _():
+        pass_on(me, shard_ref, 0, me + 2).start()
+
+    @pl.when(outer > 0)
+    def _():
+        pass_on(me, shard_ref, 1, me - 2).start()
+
+    pass_on(me, shard_ref, 2, partner).start()
+    multiply(me, shard_ref)
+    own = pltpu.make_async_copy(made.at[me], back_ref.at[me], own_sem)
+    own.start()
+
+    def arrive(source):
+        pass_on(source, held.at[source], 2, partner).wait_recv()
+
+    def take(source):
+        multiply(source, held.at[source])
+        go_home(source).start()
+
+    def step(distance, carry):
+        low, high = me - 2 * distance, me + 2 * distance
+
+        @pl.when(outer - distance >= 0)
+        def _():
+            arrive(low)
+
+            @pl.when(outer + 1 < outers)
+            def _():
+                pass_on(low, held.at[low], 0, me + 2).start()
+
+            pass_on(low, held.at[low], 2, partner).start()
+            take(low)
+
+        @pl.when(outer + distance < outers)
+        def _():
+            arrive(high)
+
+            @pl.when(outer > 0)
+            def _():
+                pass_on(high, held.at[high], 1, me - 2).start()
+
+            pass_on(high, held.at[high], 2, partner).start()
+            take(high)
+
+        for source in (
+            jnp.where(outer - (distance - 1) >= 0, partner - 2 * (distance - 1), -1),
+            jnp.where(
+                (distance > 1) & (outer + (distance - 1) < outers), partner + 2 * (distance - 1), -1
+            ),
+        ):
+
+            @pl.when(source >= 0)
+            def _():
+                arrive(source)
+                take(source)
+
+        return carry
+
+    lax.fori_loop(1, outers + 1, step, 0)
+    own.wait()
+
+    def finish(step, carry):
+        source = lax.rem(me + step, count)
+        go_home(source).wait_send()
+        pltpu.make_async_remote_copy(
+            src_ref=made.at[source],
+            dst_ref=back_ref.at[source],
+            send_sem=back_send.at[source],
+            recv_sem=back_recv.at[source],
+            device_id={"seq": source},
+            device_id_type=pl.DeviceIdType.MESH,
+        ).wait_recv()
+        return carry
+
+    lax.fori_loop(1, count, finish, 0)
+
+    def drain(step, carry):
+        source = step * 2 + inner
+
+        @pl.when((source <= me) & (outer + 1 < outers))
+        def _():
+            pass_on(source, held.at[source], 0, me + 2).wait_send()
+
+        @pl.when((source >= me) & (outer > 0))
+        def _():
+            pass_on(source, held.at[source], 1, me - 2).wait_send()
+
+        pass_on(source, held.at[source], 2, partner).wait_send()
+        return carry
+
+    lax.fori_loop(0, outers, drain, 0)
+
+
+def project(normed, out_weight):
+    count = lax.axis_size("seq")
+    rows, width = normed.shape
+    columns = out_weight.shape[1]
+    return pl.pallas_call(
+        functools.partial(project_kernel, count),
+        name="project",
+        out_shape=jax.ShapeDtypeStruct((count, rows, columns), jnp.bfloat16),
+        in_specs=[pl.BlockSpec(memory_space=pltpu.VMEM)] * 2,
+        out_specs=pl.BlockSpec(memory_space=pltpu.VMEM),
+        scratch_shapes=[
+            pltpu.VMEM((count, rows, width), jnp.bfloat16),
+            pltpu.VMEM((count, rows, columns), jnp.bfloat16),
+            pltpu.SemaphoreType.DMA((count, 3)),
+            pltpu.SemaphoreType.DMA((count,)),
+            pltpu.SemaphoreType.DMA((count,)),
+            pltpu.SemaphoreType.DMA((count,)),
+            pltpu.SemaphoreType.DMA,
+        ],
+        compiler_params=pltpu.CompilerParams(
+            collective_id=0, has_side_effects=True, vmem_limit_bytes=48 * 1024 * 1024
+        ),
+    )(normed, out_weight)
 
 
 def per_device(
@@ -75,28 +248,15 @@
         .astype(jnp.bfloat16)
         .reshape(tok_rows, local_heads * HD)
     )
-    everyone = lax.all_gather(normed, "seq", axis=0, tiled=True)
-    columns = out_weight.shape[1] // head_count
-    projected = jnp.dot(everyone, out_weight, preferred_element_type=jnp.float32)
-    kept = lax.dynamic_slice_in_dim(projected, head_pos * columns, columns, 1)
-    passed = lax.dynamic_slice_in_dim(projected, (1 - head_pos) * columns, columns, 1)
-    mine = (kept + swap_heads(passed.astype(jnp.bfloat16)).astype(jnp.float32)).astype(jnp.bfloat16)
-    mine = lax.all_to_all(
-        mine.reshape(seq_count, tok_rows, columns), "seq", 0, 0, tiled=True
-    )
-    other = swap_heads(mine)
-    first = jnp.where(head_pos == 0, mine, other)
-    second = jnp.where(head_pos == 0, other, mine)
-    attended = jnp.stack([first, second], 1).transpose(2, 0, 1, 3).reshape(tok_rows, D)
-    resid_other = swap_heads(resid)
-    resid_all = jnp.concatenate(
-        [
-            jnp.where(head_pos == 0, resid, resid_other),
-            jnp.where(head_pos == 0, resid_other, resid),
-        ],
-        axis=1,
-    )
-    hidden = (attended.astype(jnp.float32) + resid_all.astype(jnp.float32)).astype(jnp.bfloat16)
+    projected = (
+        project(normed, out_weight).transpose(1, 0, 2).reshape(tok_rows, D).astype(jnp.float32)
+    )
+    placed = lax.dynamic_update_slice_in_dim(
+        jnp.zeros((tok_rows, D), jnp.float32), resid.astype(jnp.float32), head_pos * half_width, 1
+    )
+    half = (projected + placed).astype(jnp.bfloat16)
+    other = swap_heads(half)
+    hidden = (half.astype(jnp.float32) + other.astype(jnp.float32)).astype(jnp.bfloat16)
     wide = hidden.astype(jnp.float32)
     moe_in = (
         wide * lax.rsqrt(jnp.mean(wide * wide, axis=-1, keepdims=True) + EPS) * moe_gain

time: 258 us -> 218 us (0.84)
  waiting for transfers between devices: 119 us -> 33.4 us
  Pallas kernels: 0 us -> 63.4 us
  between operations: 13.8 us -> 0.37 us
  matrix products: 35.7 us -> 30.1 us
  local copies, waits for them, and re-layouts: 8.02 us -> 12.2 us
  starting transfers between devices: 15.2 us -> 11.3 us
    all_gather x1 -> x0, waiting for transfers between devices: 73.8 us -> none  [per_device(): everyone = lax.all_gather(normed, 'seq', axis=0, tiled=True)]
    pallas_call x0 -> x1, Pallas kernels: none -> 63.4 us  [project(): pl.pallas_call(functools.partial(project_kernel, count), name='project',...]
    all_to_all x1 -> x0, waiting for transfers between devices: 9.47 us -> none  [per_device(): lax.all_to_all(mine.reshape(seq_count, tok_rows, columns), 'seq', 0, 0, t...]
    dot_general x1 -> x0, matrix products: 4.01 us -> none  [per_device(): jnp.dot(everyone, out_weight, preferred_element_type=jnp.float32)]
    all_to_all x1 -> x0, starting transfers between devices: 3.45 us -> none  [per_device(): lax.all_to_all(mine.reshape(seq_count, tok_rows, columns), 'seq', 0, 0, t...]
    ppermute x5 -> x3, waiting for transfers between devices: 6.9 us -> 5.97 us  [swap_heads(): return lax.ppermute(x, 'head', pairs)]
  transfers between devices with their start and end apart: 9 -> 5, of which waited for: 8 -> 5; matrix products, arithmetic and copies ran while one was open for 2% -> 1% of each run, Pallas kernels for 0% -> 0%
where the time goes in v2:
time: 218 us; the launch traced here: 217 us
  Pallas kernels  63.4 us (29%)
  blocking collectives  56.5 us (26%)
  waiting for transfers between devices  33.4 us (15%)
  matrix products  30.1 us (14%)
  local copies, waits for them, and re-layouts  12.2 us (6%)
  starting transfers between devices  11.3 us (5%)
  other arithmetic  10.3 us (5%)
    pallas_call x1, Pallas kernels, project(): pl.pallas_call(functools.partial(project_kernel, count), name='project',...  63.4 us
    all_to_all x1, blocking collectives, per_device(): lax.all_to_all(copies, 'seq', 0, 0, tiled=True).reshape(-1, half_width)  28.3 us
    all_to_all x1, blocking collectives, per_device(): lax.all_to_all(total.reshape(seq_count, CAP, half_width), 'seq', 0, 0, ti...  28.2 us
    all_to_all x1, waiting for transfers between devices, earlier_sums(): lax.all_to_all(own.reshape(count, own.shape[0] // count, own.shape[1]), '...  13.8 us
    all_to_all x1, waiting for transfers between devices, earlier_sums(): lax.all_to_all(jnp.stack(before), 'seq', 0, 0, tiled=True)  13.6 us
    dot_general x1, matrix products, per_device(): upward = jnp.dot(rows_in, w_up, preferred_element_type=jnp.float32)  9.34 us
    all_to_all x1, starting transfers between devices, earlier_sums(): lax.all_to_all(own.reshape(count, own.shape[0] // count, own.shape[1]), '...  7.31 us
    dot_general x1, matrix products, per_device(): jnp.dot(inner, w_down, preferred_element_type=jnp.float32)  7.13 us
  transfers between devices with their start and end apart: 5, of which 5 were waited for; matrix products, arithmetic and copies ran while one was open for 1% of the time, Pallas kernels for 0%

profile of v2, /device:TPU:0, one launch (start us, length us, event | category | flops | bytes accessed | tf_op | source)
XLA Modules:
  0.0 217.5 jit_solution(9972176456625997930)
XLA Ops:
  0.0 1.4 copy.66
  1.4 1.3 convolution_convert_fusion.2
  2.7 7.3 %all-to-all-start = ((bf16[8,256,128]{2,1,0:T(8,128)(2,1)}), bf16[8,256,128]{2,1,0:T(8,128)(2,1)S(1)}, u32[]{:S(2)}, u32[]{:S(2)}) async-start(bf16[8,256,128]{2,1,0:T(8,128)(2,1)} %bitcast), calls=%async_computation | async-start | bytes 1048576 | tf_op jit(solution)/shard_map/all_to_all | solution.py:27
  10.0 0.0 copy-start.6
  10.0 0.0 copy-start.3
  10.0 0.6 broadcast_dynamic-update-slice_fusion
  10.7 13.8 %all-to-all-done = bf16[8,256,128]{2,1,0:T(8,128)(2,1)S(1)} async-done(((bf16[8,256,128]{2,1,0:T(8,128)(2,1)}), bf16[8,256,128]{2,1,0:T(8,128)(2,1)S(1)}, u32[]{:S(2)}, u32[]{:S(2)}) %all-to-all-start) | async-done | bytes 524320 | tf_op jit(solution)/shard_map/all_to_all | solution.py:27
  24.5 0.6 slice_dynamic-update-slice_fusion
  25.1 0.6 fusion.30
  25.8 0.7 convert_dynamic-update-slice_fusion.1
  26.4 0.7 fusion.29
  27.1 0.7 convert_dynamic-update-slice_fusion
  27.8 0.6 fusion.28
  28.4 0.7 fusion.31
  29.1 3.6 %all-to-all-start.1 = ((bf16[8,256,128]{2,1,0:T(8,128)(2,1)}), bf16[8,256,128]{2,1,0:T(8,128)(2,1)S(1)}, u32[]{:S(2)}, u32[]{:S(2)}) async-start(bf16[8,256,128]{2,1,0:T(8,128)(2,1)} %fusion.31), calls=%async_computation.1 | async-start | bytes 1048576 | tf_op jit(solution)/shard_map/all_to_all | solution.py:35
  32.7 0.1 copy.61
  32.8 0.1 eq.46
  33.0 0.7 eq.42
  33.7 0.1 dynamic-slice.1
  33.8 13.6 %all-to-all-done.1 = bf16[8,256,128]{2,1,0:T(8,128)(2,1)S(1)} async-done(((bf16[8,256,128]{2,1,0:T(8,128)(2,1)}), bf16[8,256,128]{2,1,0:T(8,128)(2,1)S(1)}, u32[]{:S(2)}, u32[]{:S(2)}) %all-to-all-start.1) | async-done | bytes 524320 | tf_op jit(solution)/shard_map/all_to_all | solution.py:35
  47.4 1.5 convolution_bitcast_fusion.1
  48.9 2.1 multiply_reduce_fusion.1
  51.0 0.0 copy-start.2
  51.0 1.1 multiply_convert_fusion.2
  52.2 1.2 copy.65.shard_ref
  53.4 63.4 %project.1 = bf16[8,128,384]{2,1,0:T(8,128)(2,1)S(1)} custom-call(bf16[128,2048]{1,0:T(8,128)(2,1)S(1)} %copy.65.shard_ref, bf16[2048,384]{1,0:T(8,128)(2,1)S(1)} %copy-done.2), custom_call_target="tpu_custom_call" | custom-call | tf_op jit(solution)/shard_map/project/pallas_call | solution.py:186
  116.8 0.1 convert_bitcast_fusion
  116.9 0.5 copy.58
  117.4 0.0 copy-start.4
  117.4 0.5 copy.60
  117.9 0.5 copy-done.4
  118.4 0.1 add_dynamic-update-slice_fusion
  118.5 0.1 convert_element_type.176
  118.6 0.1 collective-permute-start
  118.7 0.6 reduce-window.6
  119.3 0.2 slice_reduce_fusion
  119.6 0.1 fusion.35
  119.7 0.1 reduce_sum.49
  119.8 0.1 copy.63
  119.9 0.1 select_reduce_fusion
  120.0 1.2 collective-permute-done
  121.1 1.4 multiply_reduce_fusion
  122.6 1.4 convolution_convert_fusion.1
  123.9 1.3 reshape_reshape.11
  125.3 28.3 %all_to_all.20 = bf16[8,36,1536]{2,1,0:T(8,128)(2,1)} all-to-all(bf16[8,36,1536]{2,1,0:T(8,128)(2,1)S(1)} %reshape_reshape.11), channel_id=1, replica_groups=mesh['grp'=2,'seq'=8,'head'=2] {'seq'}, dimensions={0} | all-to-all | bytes 1769472 | tf_op jit(solution)/shard_map/all_to_all | solution.py:284
  153.6 1.3 reshape.72
  154.9 0.1 collective-permute-start.1
  155.0 2.5 %collective-permute-done.1 = bf16[288,1536]{1,0:T(8,128)(2,1)} collective-permute-done((bf16[288,1536]{1,0:T(8,128)(2,1)S(1)}, bf16[288,1536]{1,0:T(8,128)(2,1)}, u32[]{:S(2)}, u32[]{:S(2)}) %collective-permute-start.1) | collective-permute-done | bytes 884768 | tf_op jit(solution)/shard_map/ppermute | solution.py:22
  157.5 1.4 broadcast_select_fusion.1
  159.0 0.0 slice-start.1
  159.0 0.0 slice-start.4
  159.0 9.3 %fusion.5 = f32[288,2304]{1,0:T(8,128)} fusion(bf16[3072,2304]{1,0:T(8,128)(2,1)} %param.22, bf16[288,1536]{1,0:T(8,128)(2,1)S(1)} %get-tuple-element.10, bf16[288,1536]{1,0:T(8,128)(2,1)S(1)} %get-tuple-element.9), kind=kOutput, calls=%fused_computation.18 | convolution fusion | flops 4080402432 | bytes 18579456 | tf_op jit(solution)/shard_map/dot_general | solution.py:294
  168.4 0.0 slice-start.6
  168.4 5.8 %fusion.6 = f32[288,2304]{1,0:T(8,128)} fusion(bf16[3072,2304]{1,0:T(8,128)(2,1)S(1)} %bitcast.68, bf16[288,1536]{1,0:T(8,128)(2,1)S(1)} %get-tuple-element.10, bf16[288,1536]{1,0:T(8,128)(2,1)S(1)} %get-tuple-element.9), kind=kOutput, calls=%fused_computation.19 | convolution fusion | flops 4080402432 | bytes 18579456 | tf_op jit(solution)/shard_map/dot_general | solution.py:293
  174.2 7.1 %convolution_convert_fusion = bf16[288,3072]{1,0:T(8,128)(2,1)S(1)} fusion(bf16[2304,3072]{1,0:T(8,128)(2,1)S(1)} %bitcast.70, f32[288,2304]{1,0:T(8,128)} %fusion.5, f32[288,2304]{1,0:T(8,128)} %fusion.6), kind=kOutput, calls=%fused_computation | convolution fusion | flops 4081729536 | bytes 21233664 | tf_op jit(solution)/shard_map/dot_general | solution.py:296
  181.4 0.1 constant_dynamic-slice_fusion
  181.4 0.2 collective-permute-start.2
  181.7 2.3 %collective-permute-done.2 = bf16[288,1536]{1,0:T(8,128)(2,1)S(1)} collective-permute-done((bf16[288,1536]{1,0:T(8,128)(2,1)S(1)}, bf16[288,1536]{1,0:T(8,128)(2,1)S(1)}, u32[]{:S(2)}, u32[]{:S(2)}) %collective-permute-start.2) | collective-permute-done | bytes 884768 | tf_op jit(solution)/shard_map/ppermute | solution.py:22
  183.9 1.2 add_convert_fusion
  185.1 1.3 reshape.73
  186.4 28.2 %all_to_all.21 = bf16[8,36,1536]{2,1,0:T(8,128)(2,1)} all-to-all(bf16[8,36,1536]{2,1,0:T(8,128)(2,1)S(1)} %reshape.73), channel_id=1, replica_groups=mesh['grp'=2,'seq'=8,'head'=2] {'seq'}, dimensions={0} | all-to-all | bytes 1769472 | tf_op jit(solution)/shard_map/all_to_all | solution.py:300
  214.6 1.3 reshape_squeeze_reshape.3
  215.9 0.4 fusion.33
  216.3 1.2 fusion.1
  (37 shorter events, 0.1 us)
Async XLA Ops:
  0.0 1.4 copy-start
  2.7 21.8 %all-to-all-start = ((bf16[8,256,128]{2,1,0:T(8,128)(2,1)}), bf16[8,256,128]{2,1,0:T(8,128)(2,1)S(1)}, u32[]{:S(2)}, u32[]{:S(2)}) async-start(bf16[8,256,128]{2,1,0:T(8,128)(2,1)} %bitcast), calls=%async_computation | async-start | bytes 1048576 | tf_op jit(solution)/shard_map/all_to_all | solution.py:27
  10.0 22.7 %copy-start.7 = (s32[128,2]{0,1:T(2,128)S(1)}, s32[128,2]{0,1:T(2,128)}, u32[]{:S(2)}) copy-start(s32[128,2]{0,1:T(2,128)} %param.19) | copy-start | bytes 3076
  10.0 23.7 %copy-start.6 = (f32[3072]{0:T(1024)S(1)}, f32[3072]{0:T(1024)}, u32[]{:S(2)}) copy-start(f32[3072]{0:T(1024)} %param.18) | copy-start | bytes 36868
  10.0 37.4 %copy-start.3 = (bf16[128,2048]{1,0:T(8,128)(2,1)S(1)}, bf16[128,2048]{1,0:T(8,128)(2,1)}, u32[]{:S(2)}) copy-start(bf16[128,2048]{1,0:T(8,128)(2,1)} %param.12) | copy-start | bytes 1572868
  29.1 18.3 %all-to-all-start.1 = ((bf16[8,256,128]{2,1,0:T(8,128)(2,1)}), bf16[8,256,128]{2,1,0:T(8,128)(2,1)S(1)}, u32[]{:S(2)}, u32[]{:S(2)}) async-start(bf16[8,256,128]{2,1,0:T(8,128)(2,1)} %fusion.31), calls=%async_computation.1 | async-start | bytes 1048576 | tf_op jit(solution)/shard_map/all_to_all | solution.py:35
  48.9 2.1 copy-start.5
  51.0 2.4 %copy-start.2 = (bf16[2048,384]{1,0:T(8,128)(2,1)S(1)}, bf16[2048,384]{1,0:T(8,128)(2,1)}, u32[]{:S(2)}) copy-start(bf16[2048,384]{1,0:T(8,128)(2,1)} %weight_ref.1) | copy-start | bytes 4718596
  117.4 1.0 copy-start.4
  118.4 1.2 copy-start.8
  118.4 1.5 copy-start.9
  118.6 2.5 %collective-permute-start = (bf16[128,3072]{1,0:T(8,128)(2,1)S(1)}, bf16[128,3072]{1,0:T(8,128)(2,1)}, u32[]{:S(2)}, u32[]{:S(2)}) collective-permute-start(bf16[128,3072]{1,0:T(8,128)(2,1)S(1)} %convert_element_type.176), channel_id=1, source_target_pairs={{0,1},{1,0},{2,3},{3,2},{4,5},{5,4},{6,7},{7,6},{8,9},{9,8},{10,11... | collective-permute-start | bytes 2359304 | tf_op jit(solution)/shard_map/ppermute | solution.py:22
  154.9 2.6 %collective-permute-start.1 = (bf16[288,1536]{1,0:T(8,128)(2,1)S(1)}, bf16[288,1536]{1,0:T(8,128)(2,1)}, u32[]{:S(2)}, u32[]{:S(2)}) collective-permute-start(bf16[288,1536]{1,0:T(8,128)(2,1)S(1)} %reshape.72), channel_id=1, source_target_pairs={{0,1},{1,0},{2,3},{3,2},{4,5},{5,4},{6,7},{7,6},{8,9},{9,8},{10,11... | collective-permute-start | bytes 2654216 | tf_op jit(solution)/shard_map/ppermute | solution.py:22
  157.5 10.8 %slice-start = ((s8[14155776]{0:T(1024)(128)(4,1)}), s8[4194304]{0:T(1024)(128)(4,1)S(1)}, s32[]{:S(2)}) async-start(s8[14155776]{0:T(1024)(128)(4,1)} %bitcast.67), calls=%async_computation.4 | async-start | bytes 8388608
  159.0 9.4 %slice-start.1 = ((s8[14155776]{0:T(1024)(128)(4,1)}), s8[4194304]{0:T(1024)(128)(4,1)S(1)}, s32[]{:S(2)}) async-start(s8[14155776]{0:T(1024)(128)(4,1)} %bitcast.67), calls=%async_computation.5 | async-start | bytes 8388608
  159.0 9.4 %slice-start.2 = ((s8[14155776]{0:T(1024)(128)(4,1)}), s8[4194304]{0:T(1024)(128)(4,1)S(1)}, s32[]{:S(2)}) async-start(s8[14155776]{0:T(1024)(128)(4,1)} %bitcast.67), calls=%async_computation.6 | async-start | bytes 8388608
  159.0 9.4 %slice-start.3 = ((s8[14155776]{0:T(1024)(128)(4,1)}), s8[1572864]{0:T(1024)(128)(4,1)S(1)}, s32[]{:S(2)}) async-start(s8[14155776]{0:T(1024)(128)(4,1)} %bitcast.67), calls=%async_computation.7 | async-start | bytes 3145728
  159.0 15.2 %slice-start.4 = ((s8[14155776]{0:T(1024)(128)(4,1)}), s8[4194304]{0:T(1024)(128)(4,1)S(1)}, s32[]{:S(2)}) async-start(s8[14155776]{0:T(1024)(128)(4,1)} %bitcast.69), calls=%async_computation.8 | async-start | bytes 8388608
  159.0 15.2 %slice-start.5 = ((s8[14155776]{0:T(1024)(128)(4,1)}), s8[4194304]{0:T(1024)(128)(4,1)S(1)}, s32[]{:S(2)}) async-start(s8[14155776]{0:T(1024)(128)(4,1)} %bitcast.69), calls=%async_computation.9 | async-start | bytes 8388608
  168.4 5.8 %slice-start.6 = ((s8[14155776]{0:T(1024)(128)(4,1)}), s8[4194304]{0:T(1024)(128)(4,1)S(1)}, s32[]{:S(2)}) async-start(s8[14155776]{0:T(1024)(128)(4,1)} %bitcast.69), calls=%async_computation.10 | async-start | bytes 8388608
  168.4 5.8 %slice-start.7 = ((s8[14155776]{0:T(1024)(128)(4,1)}), s8[1572864]{0:T(1024)(128)(4,1)S(1)}, s32[]{:S(2)}) async-start(s8[14155776]{0:T(1024)(128)(4,1)} %bitcast.69), calls=%async_computation.11 | async-start | bytes 3145728
  181.4 2.5 %collective-permute-start.2 = (bf16[288,1536]{1,0:T(8,128)(2,1)S(1)}, bf16[288,1536]{1,0:T(8,128)(2,1)S(1)}, u32[]{:S(2)}, u32[]{:S(2)}) collective-permute-start(bf16[288,1536]{1,0:T(8,128)(2,1)S(1)} %constant_dynamic-slice_fusion), channel_id=1, source_target_pairs={{0,1},{1,0},{2,3},{3,2},{4,5},{5,4},{6,7},{7,6},{8,9},{9,8},{10,11... | collective-permute-start | bytes 2654216 | tf_op jit(solution)/shard_map/ppermute | solution.py:22
  215.9 1.6 copy-start.1

commit v3 on v2

--- a/solution.py
+++ b/solution.py
@@ -22,20 +22,7 @@
     return lax.ppermute(x, "head", pairs)
 
 
-def earlier_sums(own):
-    count = lax.axis_size("seq")
-    blocks = lax.all_to_all(
-        own.reshape(count, own.shape[0] // count, own.shape[1]), "seq", 0, 0, tiled=True
-    )
-    running = jnp.zeros(blocks.shape[1:], jnp.float32)
-    before = []
-    for k in range(count):
-        before.append(running.astype(jnp.bfloat16))
-        running = running + blocks[k].astype(jnp.float32)
-    return lax.all_to_all(jnp.stack(before), "seq", 0, 0, tiled=True).reshape(own.shape)
-
-
-def greet_all(me, count):
+def greet_all(me, count, pair=False):
     barrier = pltpu.get_barrier_semaphore()
 
     def greet(step, carry):
@@ -48,7 +35,251 @@
         return carry
 
     lax.fori_loop(1, count, greet, 0)
-    pl.semaphore_wait(barrier, count - 1)
+    if pair:
+        pl.semaphore_signal(
+            barrier,
+            inc=1,
+            device_id={"head": 1 - lax.axis_index("head")},
+            device_id_type=pl.DeviceIdType.MESH,
+        )
+    pl.semaphore_wait(barrier, count - 1 + int(pair))
+
+
+def send_to(src, dst, send_sem, recv_sem, **device):
+    return pltpu.make_async_remote_copy(
+        src_ref=src,
+        dst_ref=dst,
+        send_sem=send_sem,
+        recv_sem=recv_sem,
+        device_id=device,
+        device_id_type=pl.DeviceIdType.MESH,
+    )
+
+
+def sums_kernel(count, own_ref, out_ref, got, made, send_sem, recv_sem, home_send, home_recv):
+    me = lax.axis_index("seq")
+    greet_all(me, count)
+
+    def out(other):
+        return send_to(
+            own_ref.at[other], got.at[me], send_sem.at[other], recv_sem.at[me], seq=other
+        )
+
+    def arrival(other):
+        return send_to(
+            own_ref.at[other], got.at[other], send_sem.at[other], recv_sem.at[other], seq=other
+        )
+
+    def home(other):
+        return send_to(
+            made.at[other], out_ref.at[me], home_send.at[other], home_recv.at[me], seq=other
+        )
+
+    def home_arrival(other):
+        return send_to(
+            made.at[other], out_ref.at[other], home_send.at[other], home_recv.at[other], seq=other
+        )
+
+    def start(step, carry):
+        out(lax.rem(me + step, count)).start()
+        return carry
+
+    lax.fori_loop(1, count, start, 0)
+    got[me] = own_ref[me]
+
+    def add(block, running):
+        made[block] = running.astype(jnp.bfloat16)
+
+        @pl.when(block != me)
+        def _():
+            arrival(block).wait_recv()
+            home(block).start()
+
+        return running + got[block].astype(jnp.float32)
+
+    lax.fori_loop(0, count, add, jnp.zeros(got.shape[1:], jnp.float32))
+    out_ref[me] = made[me]
+
+    def finish(step, carry):
+        other = lax.rem(me + step, count)
+        out(other).wait_send()
+        home_arrival(other).wait_recv()
+        home(other).wait_send()
+        return carry
+
+    lax.fori_loop(1, count, finish, 0)
+
+
+def earlier_sums(own):
+    count = lax.axis_size("seq")
+    shape = (count, own.shape[0] // count, own.shape[1])
+    return pl.pallas_call(
+        functools.partial(sums_kernel, count),
+        name="sums",
+        out_shape=jax.ShapeDtypeStruct(shape, jnp.bfloat16),
+        in_specs=[pl.BlockSpec(memory_space=pltpu.VMEM)],
+        out_specs=pl.BlockSpec(memory_space=pltpu.VMEM),
+        scratch_shapes=[pltpu.VMEM(shape, jnp.bfloat16)] * 2
+        + [pltpu.SemaphoreType.DMA((count,))] * 4,
+        compiler_params=pltpu.CompilerParams(
+            collective_id=1, has_side_effects=True, vmem_limit_bytes=16 * 1024 * 1024
+        ),
+    )(own.reshape(shape)).reshape(own.shape)
+
+
+def dispatch_kernel(
+    count, packed_ref, rows_ref, send_sem, recv_sem, pair_send, pair_recv, own_sem
+):
+    me, head = lax.axis_index("seq"), lax.axis_index("head")
+    half = packed_ref.shape[2]
+    greet_all(me, count, True)
+
+    def place(source, side):
+        return rows_ref.at[source, :, pl.ds(pl.multiple_of(side * half, 128), half)]
+
+    def out(other):
+        return send_to(
+            packed_ref.at[other], place(me, head), send_sem.at[other], recv_sem.at[me], seq=other
+        )
+
+    def arrival(other):
+        return send_to(
+            packed_ref.at[other],
+            place(other, head),
+            send_sem.at[other],
+            recv_sem.at[other],
+            seq=other,
+        )
+
+    def pair(source, src, side):
+        return send_to(
+            src, place(source, side), pair_send.at[source], pair_recv.at[source], head=1 - head
+        )
+
+    def start(step, carry):
+        out(lax.rem(me + step, count)).start()
+        return carry
+
+    lax.fori_loop(1, count, start, 0)
+    own = pltpu.make_async_copy(packed_ref.at[me], place(me, head), own_sem)
+    own.start()
+    pair(me, packed_ref.at[me], head).start()
+
+    def hand_on(step, carry):
+        source = lax.rem(me - step + count, count)
+        arrival(source).wait_recv()
+        pair(source, place(source, head), head).start()
+        return carry
+
+    lax.fori_loop(1, count, hand_on, 0)
+    own.wait()
+
+    def finish(source, carry):
+        pair(source, place(source, head), head).wait_send()
+        pair(source, place(source, 1 - head), 1 - head).wait_recv()
+
+        @pl.when(source != me)
+        def _():
+            out(source).wait_send()
+
+        return carry
+
+    lax.fori_loop(0, count, finish, 0)
+
+
+def dispatch(packed):
+    count, slots, half = packed.shape
+    return pl.pallas_call(
+        functools.partial(dispatch_kernel, count),
+        name="dispatch",
+        out_shape=jax.ShapeDtypeStruct((count, slots, 2 * half), jnp.bfloat16),
+        in_specs=[pl.BlockSpec(memory_space=pltpu.VMEM)],
+        out_specs=pl.BlockSpec(memory_space=pltpu.VMEM),
+        scratch_shapes=[pltpu.SemaphoreType.DMA((count,))] * 4 + [pltpu.SemaphoreType.DMA],
+        compiler_params=pltpu.CompilerParams(
+            collective_id=2, has_side_effects=True, vmem_limit_bytes=32 * 1024 * 1024
+        ),
+    )(packed)
+
+
+def combine_kernel(
+    count, part_ref, back_ref, theirs, total, send_sem, recv_sem, pair_send, pair_recv
+):
+    me, head = lax.axis_index("seq"), lax.axis_index("head")
+    half = back_ref.shape[2]
+    greet_all(me, count, True)
+
+    def pair(block):
+        columns = pl.ds(pl.multiple_of((1 - head) * half, 128), half)
+        return send_to(
+            part_ref.at[block, :, columns],
+            theirs.at[block],
+            pair_send.at[block],
+            pair_recv.at[block],
+            head=1 - head,
+        )
+
+    def home(other):
+        return send_to(
+            total.at[other], back_ref.at[me], send_sem.at[other], recv_sem.at[me], seq=other
+        )
+
+    def home_arrival(other):
+        return send_to(
+            total.at[other], back_ref.at[other], send_sem.at[other], recv_sem.at[other], seq=other
+        )
+
+    def start(step, carry):
+        pair(lax.rem(me + step, count)).start()
+        return carry
+
+    lax.fori_loop(1, count + 1, start, 0)
+    kept = pl.ds(pl.multiple_of(head * half, 128), half)
+
+    def add(step, carry):
+        block = lax.rem(me + step, count)
+        pair(block).wait_recv()
+        total[block] = (
+            part_ref[block, :, kept].astype(jnp.float32) + theirs[block].astype(jnp.float32)
+        ).astype(jnp.bfloat16)
+
+        @pl.when(block != me)
+        def _():
+            home(block).start()
+
+        return carry
+
+    lax.fori_loop(1, count + 1, add, 0)
+    back_ref[me] = total[me]
+
+    def finish(block, carry):
+        pair(block).wait_send()
+
+        @pl.when(block != me)
+        def _():
+            home_arrival(block).wait_recv()
+            home(block).wait_send()
+
+        return carry
+
+    lax.fori_loop(0, count, finish, 0)
+
+
+def combine(part):
+    count, slots, width = part.shape
+    shape = (count, slots, width // 2)
+    return pl.pallas_call(
+        functools.partial(combine_kernel, count),
+        name="combine",
+        out_shape=jax.ShapeDtypeStruct(shape, jnp.bfloat16),
+        in_specs=[pl.BlockSpec(memory_space=pltpu.VMEM)],
+        out_specs=pl.BlockSpec(memory_space=pltpu.VMEM),
+        scratch_shapes=[pltpu.VMEM(shape, jnp.bfloat16)] * 2
+        + [pltpu.SemaphoreType.DMA((count,))] * 4,
+        compiler_params=pltpu.CompilerParams(
+            collective_id=3, has_side_effects=True, vmem_limit_bytes=40 * 1024 * 1024
+        ),
+    )(part)
 
 
 def project_kernel(
@@ -281,25 +512,12 @@
     copies = jnp.broadcast_to(
         packed.reshape(EXPERTS, 1, CAP, half_width), (EXPERTS, chips, CAP, half_width)
     ).reshape(EXPERTS * chips, CAP, half_width)
-    received = lax.all_to_all(copies, "seq", 0, 0, tiled=True).reshape(-1, half_width)
-    partner = swap_heads(received)
-    rows_in = jnp.concatenate(
-        [
-            jnp.where(head_pos == 0, received, partner),
-            jnp.where(head_pos == 0, partner, received),
-        ],
-        axis=1,
-    )
+    rows_in = dispatch(copies).reshape(-1, D)
     gate = jnp.dot(rows_in, w_gate, preferred_element_type=jnp.float32)
     upward = jnp.dot(rows_in, w_up, preferred_element_type=jnp.float32)
     inner = (jax.nn.silu(gate) * upward).astype(jnp.bfloat16)
     part = jnp.dot(inner, w_down, preferred_element_type=jnp.float32).astype(jnp.bfloat16)
-    kept = lax.dynamic_slice_in_dim(part, head_pos * half_width, half_width, 1)
-    passed = lax.dynamic_slice_in_dim(part, (1 - head_pos) * half_width, half_width, 1)
-    total = (kept.astype(jnp.float32) + swap_heads(passed).astype(jnp.float32)).astype(jnp.bfloat16)
-    back = lax.all_to_all(
-        total.reshape(seq_count, CAP, half_width), "seq", 0, 0, tiled=True
-    ).reshape(EXPERTS, chips, CAP, half_width)
+    back = combine(part.reshape(seq_count, CAP, D)).reshape(EXPERTS, chips, CAP, half_width)
     high = combine_weights.astype(jnp.bfloat16)
     low = (combine_weights - high.astype(jnp.float32)).astype(jnp.bfloat16)
     moe_out = jnp.zeros((tok_rows, half_width), jnp.float32)

time: 218 us -> 196 us (0.90)
  the two profiles are of different devices: /device:TPU:0 before, /device:TPU:15 now
where the time goes in v3:
time: 196 us; the launch traced here: 195 us
  Pallas kernels  140 us (71%)
  matrix products  36.7 us (19%)
  local copies, waits for them, and re-layouts  10.5 us (5%)
  starting transfers between devices  4.5 us (2%)
  other arithmetic  3.47 us (2%)
    pallas_call x1, Pallas kernels, project(): pl.pallas_call(functools.partial(project_kernel, count), name='project',...  55.7 us
    pallas_call x1, Pallas kernels, dispatch(): pl.pallas_call(functools.partial(dispatch_kernel, count), name='dispatch'...  28.7 us
    pallas_call x1, Pallas kernels, earlier_sums(): pl.pallas_call(functools.partial(sums_kernel, count), name='sums', out_sh...  27.6 us
    pallas_call x1, Pallas kernels, combine(): pl.pallas_call(functools.partial(combine_kernel, count), name='combine',...  27.5 us
    dot_general x1, matrix products, per_device(): jnp.dot(inner, w_down, preferred_element_type=jnp.float32)  20.3 us
    dot_general x1, matrix products, per_device(): gate = jnp.dot(rows_in, w_gate, preferred_element_type=jnp.float32)  11.5 us
    ppermute x1, starting transfers between devices, swap_heads(): return lax.ppermute(x, 'head', pairs)  4.5 us
  transfers between devices with their start and end apart: 1, of which 1 were waited for; matrix products, arithmetic and copies ran while one was open for 1% of the time, Pallas kernels for 0%

profile of v3, /device:TPU:15, one launch (start us, length us, event | category | flops | bytes accessed | tf_op | source)
XLA Modules:
  0.0 195.4 jit_solution(3106564556162474330)
XLA Ops:
  0.0 0.0 copy-start
  0.0 0.0 copy-start.5
  0.0 1.4 copy.67
  1.4 0.0 copy-done
  1.4 0.5 convolution_convert_fusion.2
  2.0 27.6 %sums.1 = bf16[8,256,128]{2,1,0:T(8,128)(2,1)S(1)} custom-call(bf16[8,256,128]{2,1,0:T(8,128)(2,1)S(1)} %bitcast.63), custom_call_target="tpu_custom_call" | custom-call | tf_op jit(solution)/shard_map/sums/pallas_call | solution.py:116
  29.6 0.0 copy-done.5
  29.6 0.5 convolution_bitcast_fusion.1
  30.1 0.0 copy-start.8
  30.1 1.9 multiply_reduce_fusion.1
  32.0 0.0 copy-start.2
  32.0 0.0 copy-done.8
  32.1 1.1 multiply_convert_fusion
  33.2 1.2 copy.66.shard_ref
  34.4 0.0 copy-done.2
  34.4 55.7 %project.1 = bf16[8,128,384]{2,1,0:T(8,128)(2,1)S(1)} custom-call(bf16[128,2048]{1,0:T(8,128)(2,1)S(1)} %copy.66.shard_ref, bf16[2048,384]{1,0:T(8,128)(2,1)S(1)} %copy-done.2), custom_call_target="tpu_custom_call" | custom-call | tf_op jit(solution)/shard_map/project/pallas_call | solution.py:417
  90.1 0.1 convert_bitcast_fusion
  90.3 0.5 copy.59
  90.7 0.0 copy-start.7
  90.7 0.5 copy.61
  91.2 0.5 copy-done.7
  91.7 0.0 copy-start.10
  91.7 0.1 add_dynamic-update-slice_fusion
  91.9 0.0 copy-start.9
  91.9 0.0 copy-start.11
  91.9 1.0 convert_element_type.81
  92.9 4.5 %collective-permute-start = (bf16[128,3072]{1,0:T(8,128)(2,1)}, bf16[128,3072]{1,0:T(8,128)(2,1)S(1)}, u32[]{:S(2)}, u32[]{:S(2)}) collective-permute-start(bf16[128,3072]{1,0:T(8,128)(2,1)} %convert_element_type.81), channel_id=1, source_target_pairs={{0,1},{1,0},{2,3},{3,2},{4,5},{5,4},{6,7},{7,6},{8,9},{9,8},{10,11... | collective-permute-start | bytes 2359304 | tf_op jit(solution)/shard_map/ppermute | solution.py:22
  97.4 0.0 copy-done.10
  97.4 0.1 copy.62
  97.5 0.1 eq.42
  97.6 0.1 eq.38
  97.8 0.0 copy-done.9
  97.8 0.1 dynamic-slice.1
  97.9 0.6 reduce-window.6
  98.4 0.2 slice_reduce_fusion
  98.7 0.1 fusion.26
  98.8 0.1 reduce_sum.49
  98.9 0.1 copy.64
  99.0 0.0 copy-done.11
  99.0 0.1 select_reduce_fusion
  99.1 0.4 collective-permute-done
  99.5 0.3 multiply_reduce_fusion
  99.8 0.0 copy-start.3
  99.8 1.2 copy-done.3
  101.0 0.5 convolution_convert_fusion.1
  101.5 0.2 reshape_reshape.11.packed_ref
  101.6 28.7 %dispatch.1 = bf16[8,36,3072]{2,1,0:T(8,128)(2,1)S(1)} custom-call(bf16[8,36,1536]{2,1,0:T(8,128)(2,1)S(1)} %reshape_reshape.11.packed_ref), custom_call_target="tpu_custom_call" | custom-call | tf_op jit(solution)/shard_map/dispatch/pallas_call | solution.py:192
  130.4 1.4 reshape.71
  131.8 0.0 copy-start.6
  131.8 11.5 %fusion.35 = f32[288,2304]{1,0:T(8,128)} fusion(bf16[288,3072]{1,0:T(8,128)(2,1)} %reshape.71, bf16[3072,2304]{1,0:T(8,128)(2,1)} %param.21), kind=kOutput, calls=%fused_computation.54 | convolution fusion | flops 4076863488 | bytes 18579456 | tf_op jit(solution)/shard_map/dot_general | solution.py:516
  143.3 0.0 copy-done.6
  143.3 20.3 %convolution_convert_fusion = bf16[288,3072]{1,0:T(8,128)(2,1)} fusion(bf16[2304,3072]{1,0:T(8,128)(2,1)} %param.23, bf16[288,3072]{1,0:T(8,128)(2,1)S(1)} %copy-done.6, bf16[3072,2304]{1,0:T(8,128)(2,1)} %param.22, f32[288,2304]{1,0:T(8,128)} %fusion.35), kind=kOutput, calls=%fused_computation.2 | convolution fusion | flops 8158593024 | bytes 34504704 | tf_op jit(solution)/shard_map/dot_general | solution.py:519
  163.6 1.6 reshape.72.part_ref
  165.2 27.5 %combine.1 = bf16[8,36,1536]{2,1,0:T(8,128)(2,1)S(1)} custom-call(bf16[8,36,3072]{2,1,0:T(8,128)(2,1)S(1)} %reshape.72.part_ref), custom_call_target="tpu_custom_call" | custom-call | tf_op jit(solution)/shard_map/combine/pallas_call | solution.py:271
  192.7 0.2 reshape_squeeze_reshape.3
  192.8 0.0 copy-start.4
  192.8 0.0 copy-start.1
  192.8 0.4 fusion.24
  193.2 1.0 copy-done.4
  194.2 1.1 fusion.2
  195.4 0.0 copy-done.1
  (7 shorter events, 0.1 us)
Async XLA Ops:
  0.0 1.4 copy-start
  0.0 29.5 %copy-start.5 = (bf16[128,2048]{1,0:T(8,128)(2,1)S(1)}, bf16[128,2048]{1,0:T(8,128)(2,1)}, u32[]{:S(2)}) copy-start(bf16[128,2048]{1,0:T(8,128)(2,1)} %param.12) | copy-start | bytes 1572868
  30.1 1.9 copy-start.8
  32.0 2.4 %copy-start.2 = (bf16[2048,384]{1,0:T(8,128)(2,1)S(1)}, bf16[2048,384]{1,0:T(8,128)(2,1)}, u32[]{:S(2)}) copy-start(bf16[2048,384]{1,0:T(8,128)(2,1)} %weight_ref.1) | copy-start | bytes 4718596
  90.7 1.0 copy-start.7
  91.7 5.6 %copy-start.10 = (s32[128,2]{0,1:T(2,128)S(1)}, s32[128,2]{0,1:T(2,128)}, u32[]{:S(2)}) copy-start(s32[128,2]{0,1:T(2,128)} %param.19) | copy-start | bytes 3076
  91.9 5.9 %copy-start.9 = (f32[3072]{0:T(1024)S(1)}, f32[3072]{0:T(1024)}, u32[]{:S(2)}) copy-start(f32[3072]{0:T(1024)} %param.18) | copy-start | bytes 36868
  91.9 7.1 %copy-start.11 = (f32[128,2]{0,1:T(2,128)S(1)}, f32[128,2]{0,1:T(2,128)}, u32[]{:S(2)}) copy-start(f32[128,2]{0,1:T(2,128)} %param.20) | copy-start | bytes 3076
  92.9 6.6 %collective-permute-start = (bf16[128,3072]{1,0:T(8,128)(2,1)}, bf16[128,3072]{1,0:T(8,128)(2,1)S(1)}, u32[]{:S(2)}, u32[]{:S(2)}) collective-permute-start(bf16[128,3072]{1,0:T(8,128)(2,1)} %convert_element_type.81), channel_id=1, source_target_pairs={{0,1},{1,0},{2,3},{3,2},{4,5},{5,4},{6,7},{7,6},{8,9},{9,8},{10,11... | collective-permute-start | bytes 2359304 | tf_op jit(solution)/shard_map/ppermute | solution.py:22
  99.8 1.2 copy-start.3
  131.8 11.5 %copy-start.6 = (bf16[288,3072]{1,0:T(8,128)(2,1)S(1)}, bf16[288,3072]{1,0:T(8,128)(2,1)}, u32[]{:S(2)}) copy-start(bf16[288,3072]{1,0:T(8,128)(2,1)} %reshape.71) | copy-start | bytes 5308420
  192.8 1.4 copy-start.4
  192.8 2.5 %copy-start.1 = (bf16[128,2048]{1,0:T(8,128)(2,1)S(1)}, bf16[128,2048]{1,0:T(8,128)(2,1)}, u32[]{:S(2)}) copy-start(bf16[128,2048]{1,0:T(8,128)(2,1)} %param.13) | copy-start | bytes 1572868

commit v4 on v3

--- a/solution.py
+++ b/solution.py
@@ -43,6 +43,16 @@
             device_id_type=pl.DeviceIdType.MESH,
         )
     pl.semaphore_wait(barrier, count - 1 + int(pair))
+
+
+def grant(*blocks):
+    total = 1 << 20
+    for shape in blocks:
+        cells = (-(-shape[-1] // 128) * 128) * (-(-shape[-2] // 16) * 16)
+        for size in shape[:-2]:
+            cells = cells * size
+        total = total + 2 * cells
+    return total
 
 
 def send_to(src, dst, send_sem, recv_sem, **device):
@@ -122,7 +132,7 @@
         scratch_shapes=[pltpu.VMEM(shape, jnp.bfloat16)] * 2
         + [pltpu.SemaphoreType.DMA((count,))] * 4,
         compiler_params=pltpu.CompilerParams(
-            collective_id=1, has_side_effects=True, vmem_limit_bytes=16 * 1024 * 1024
+            collective_id=1, has_side_effects=True, vmem_limit_bytes=grant(shape, shape, shape, shape, shape)
         ),
     )(own.reshape(shape)).reshape(own.shape)
 
@@ -197,7 +207,7 @@
         out_specs=pl.BlockSpec(memory_space=pltpu.VMEM),
         scratch_shapes=[pltpu.SemaphoreType.DMA((count,))] * 4 + [pltpu.SemaphoreType.DMA],
         compiler_params=pltpu.CompilerParams(
-            collective_id=2, has_side_effects=True, vmem_limit_bytes=32 * 1024 * 1024
+            collective_id=2, has_side_effects=True, vmem_limit_bytes=grant((count, slots, 3 * half))
         ),
     )(packed)
 
@@ -277,7 +287,7 @@
         scratch_shapes=[pltpu.VMEM(shape, jnp.bfloat16)] * 2
         + [pltpu.SemaphoreType.DMA((count,))] * 4,
         compiler_params=pltpu.CompilerParams(
-            collective_id=3, has_side_effects=True, vmem_limit_bytes=40 * 1024 * 1024
+            collective_id=3, has_side_effects=True, vmem_limit_bytes=grant(shape, shape, shape, part.shape, shape[1:])
         ),
     )(part)
 
@@ -430,7 +440,11 @@
             pltpu.SemaphoreType.DMA,
         ],
         compiler_params=pltpu.CompilerParams(
-            collective_id=0, has_side_effects=True, vmem_limit_bytes=48 * 1024 * 1024
+            collective_id=0,
+            has_side_effects=True,
+            vmem_limit_bytes=grant(
+                (count + 1, rows, width), (2 * count + 8, rows, columns), out_weight.shape
+            ),
         ),
     )(normed, out_weight)
 
@@ -516,6 +530,7 @@
     gate = jnp.dot(rows_in, w_gate, preferred_element_type=jnp.float32)
     upward = jnp.dot(rows_in, w_up, preferred_element_type=jnp.float32)
     inner = (jax.nn.silu(gate) * upward).astype(jnp.bfloat16)
+    inner = lax.optimization_barrier(inner)
     part = jnp.dot(inner, w_down, preferred_element_type=jnp.float32).astype(jnp.bfloat16)
     back = combine(part.reshape(seq_count, CAP, D)).reshape(EXPERTS, chips, CAP, half_width)
     high = combine_weights.astype(jnp.bfloat16)

time: 196 us -> 188 us (0.959)
  matrix products: 36.7 us -> 28.8 us
    dot_general x1, matrix products: 20.3 us -> 5.55 us  [per_device(): jnp.dot(inner, w_down, preferred_element_type=jnp.float32)]
    dot_general x0 -> x1, matrix products: none -> 9.59 us  [per_device(): upward = jnp.dot(rows_in, w_up, preferred_element_type=jnp.float32)]
    dot_general x1, matrix products: 11.5 us -> 8.75 us  [per_device(): gate = jnp.dot(rows_in, w_gate, preferred_element_type=jnp.float32)]
where the time goes in v4:
time: 188 us
  Pallas kernels  140 us (74%)
  matrix products  28.8 us (15%)
  local copies, waits for them, and re-layouts  10.6 us (6%)
  starting transfers between devices  4.5 us (2%)
  other arithmetic  3.48 us (2%)
    pallas_call x1, Pallas kernels, project(): pl.pallas_call(functools.partial(project_kernel, count), name='project',...  55.7 us
    pallas_call x1, Pallas kernels, dispatch(): pl.pallas_call(functools.partial(dispatch_kernel, count), name='dispatch'...  28.8 us
    pallas_call x1, Pallas kernels, earlier_sums(): pl.pallas_call(functools.partial(sums_kernel, count), name='sums', out_sh...  27.6 us
    pallas_call x1, Pallas kernels, combine(): pl.pallas_call(functools.partial(combine_kernel, count), name='combine',...  27.5 us
    dot_general x1, matrix products, per_device(): upward = jnp.dot(rows_in, w_up, preferred_element_type=jnp.float32)  9.59 us
    dot_general x1, matrix products, per_device(): gate = jnp.dot(rows_in, w_gate, preferred_element_type=jnp.float32)  8.75 us
    dot_general x1, matrix products, per_device(): jnp.dot(inner, w_down, preferred_element_type=jnp.float32)  5.55 us
    ppermute x1, starting transfers between devices, swap_heads(): return lax.ppermute(x, 'head', pairs)  4.5 us
  transfers between devices with their start and end apart: 1, of which 1 were waited for; matrix products, arithmetic and copies ran while one was open for 1% of the time, Pallas kernels for 0%

profile of v4, /device:TPU:15, one launch (start us, length us, event | category | flops | bytes accessed | tf_op | source)
XLA Modules:
  0.0 187.6 jit_solution(8764536744116869208)
XLA Ops:
  0.0 0.0 copy-start
  0.0 0.0 copy-start.5
  0.0 1.4 copy.67
  1.4 0.0 copy-done
  1.4 0.5 convolution_convert_fusion.2
  2.0 27.6 %sums.1 = bf16[8,256,128]{2,1,0:T(8,128)(2,1)S(1)} custom-call(bf16[8,256,128]{2,1,0:T(8,128)(2,1)S(1)} %bitcast.64), custom_call_target="tpu_custom_call" | custom-call | tf_op jit(solution)/shard_map/sums/pallas_call | solution.py:126
  29.6 0.0 copy-done.5
  29.6 0.5 convolution_bitcast_fusion.1
  30.1 1.9 %multiply_reduce_fusion.1 = (f32[128,16]{0,1:T(8,128)S(1)}, f32[128,16,128]{0,2,1:T(8,128)S(1)}) fusion(f32[128,16,128]{0,2,1:T(8,128)S(1)} %convolution_bitcast_fusion.1, bf16[128,16,128]{0,2,1:T(8,128)(2,1)S(1)} %bitcast.68, pred[128,128]{1,0:T(8,128)(4,1)S(1)} %iota_compare_fusion.1, bf16[128,2048]{1,0:T(8,128)(2,1)} %param.12, ...), kind=kOutput, calls=%fused_computation.17 | convolution fusion | flops 135526400 | bytes 3694592 | tf_op jit(solution)/shard_map/rbj,jrh->brh/dot_general | solution.py:486
  32.0 0.0 copy-start.2
  32.0 0.0 copy-done.8
  32.1 1.1 multiply_convert_fusion
  33.2 1.2 copy.66.shard_ref
  34.4 0.0 copy-done.2
  34.4 55.7 %project.1 = bf16[8,128,384]{2,1,0:T(8,128)(2,1)S(1)} custom-call(bf16[128,2048]{1,0:T(8,128)(2,1)S(1)} %copy.66.shard_ref, bf16[2048,384]{1,0:T(8,128)(2,1)S(1)} %copy-done.2), custom_call_target="tpu_custom_call" | custom-call | tf_op jit(solution)/shard_map/project/pallas_call | solution.py:427
  90.1 0.1 convert_bitcast_fusion
  90.3 0.5 copy.59
  90.7 0.0 copy-start.7
  90.7 0.5 copy.61
  91.2 0.5 copy-done.7
  91.7 0.1 add_dynamic-update-slice_fusion
  91.9 0.0 copy-start.9
  91.9 0.0 copy-start.11
  91.9 1.0 convert_element_type.81
  92.9 4.5 %collective-permute-start = (bf16[128,3072]{1,0:T(8,128)(2,1)}, bf16[128,3072]{1,0:T(8,128)(2,1)S(1)}, u32[]{:S(2)}, u32[]{:S(2)}) collective-permute-start(bf16[128,3072]{1,0:T(8,128)(2,1)} %convert_element_type.81), channel_id=1, source_target_pairs={{0,1},{1,0},{2,3},{3,2},{4,5},{5,4},{6,7},{7,6},{8,9},{9,8},{10,11... | collective-permute-start | bytes 2359304 | tf_op jit(solution)/shard_map/ppermute | solution.py:22
  97.4 0.0 copy-done.10
  97.4 0.1 copy.62
  97.5 0.1 eq.42
  97.6 0.1 eq.38
  97.8 0.0 copy-done.9
  97.8 0.1 dynamic-slice.1
  97.9 0.6 reduce-window.6
  98.4 0.2 slice_reduce_fusion
  98.7 0.1 fusion.26
  98.8 0.1 reduce_sum.49
  98.9 0.1 copy.64
  99.0 0.0 copy-done.11
  99.0 0.1 select_reduce_fusion
  99.1 0.4 collective-permute-done
  99.5 0.3 multiply_reduce_fusion
  99.8 0.0 copy-start.3
  99.8 1.1 copy-done.3
  101.0 0.5 convolution_convert_fusion.1
  101.4 0.2 reshape_reshape.11.packed_ref
  101.6 28.8 %dispatch.1 = bf16[8,36,3072]{2,1,0:T(8,128)(2,1)S(1)} custom-call(bf16[8,36,1536]{2,1,0:T(8,128)(2,1)S(1)} %reshape_reshape.11.packed_ref), custom_call_target="tpu_custom_call" | custom-call | tf_op jit(solution)/shard_map/dispatch/pallas_call | solution.py:202
  130.4 1.4 reshape.71
  131.8 8.7 %fusion.34 = f32[288,2304]{1,0:T(8,128)S(1)} fusion(bf16[288,3072]{1,0:T(8,128)(2,1)} %reshape.71, bf16[3072,2304]{1,0:T(8,128)(2,1)} %param.21), kind=kOutput, calls=%fused_computation.53 | convolution fusion | flops 4076863488 | bytes 18579456 | tf_op jit(solution)/shard_map/dot_general | solution.py:530
  140.6 0.0 copy-done.6
  140.6 0.0 slice-start.2
  140.6 0.0 slice-start.3
  140.6 9.6 %fusion = bf16[288,2304]{1,0:T(8,128)(2,1)S(1)} fusion(bf16[288,3072]{1,0:T(8,128)(2,1)S(1)} %copy-done.6, bf16[3072,2304]{1,0:T(8,128)(2,1)} %param.22, f32[288,2304]{1,0:T(8,128)S(1)} %fusion.34), kind=kOutput, calls=%fused_computation.1 | convolution fusion | flops 4080844800 | bytes 19906560 | tf_op jit(solution)/shard_map/dot_general | solution.py:531
  150.2 0.0 slice-done
  150.2 0.0 slice-done.1
  150.2 0.0 slice-done.2
  150.2 0.0 slice-done.3
  150.2 5.6 %convolution_convert_fusion = bf16[288,3072]{1,0:T(8,128)(2,1)} fusion(bf16[288,2304]{1,0:T(8,128)(2,1)S(1)} %fusion, bf16[2304,3072]{1,0:T(8,128)(2,1)S(1)} %bitcast.72), kind=kOutput, calls=%fused_computation.2 | convolution fusion | flops 4077748224 | bytes 17252352 | tf_op jit(solution)/shard_map/dot_general | solution.py:534
  155.8 1.6 reshape.72.part_ref
  157.4 27.5 %combine.1 = bf16[8,36,1536]{2,1,0:T(8,128)(2,1)S(1)} custom-call(bf16[8,36,3072]{2,1,0:T(8,128)(2,1)S(1)} %reshape.72.part_ref), custom_call_target="tpu_custom_call" | custom-call | tf_op jit(solution)/shard_map/combine/pallas_call | solution.py:281
  184.9 0.2 reshape_squeeze_reshape.3
  185.1 0.0 copy-start.4
  185.1 0.0 copy-start.1
  185.1 0.4 fusion.24
  185.5 1.0 copy-done.4
  186.5 1.1 fusion.2
  (14 shorter events, 0.1 us)
Async XLA Ops:
  0.0 1.4 copy-start
  0.0 29.5 %copy-start.5 = (bf16[128,2048]{1,0:T(8,128)(2,1)S(1)}, bf16[128,2048]{1,0:T(8,128)(2,1)}, u32[]{:S(2)}) copy-start(bf16[128,2048]{1,0:T(8,128)(2,1)} %param.12) | copy-start | bytes 1572868
  30.1 1.9 %copy-start.8 = (f32[2048]{0:T(1024)S(1)}, f32[2048]{0:T(1024)}, u32[]{:S(2)}) copy-start(f32[2048]{0:T(1024)} %param.16) | copy-start | bytes 24580
  32.0 2.4 %copy-start.2 = (bf16[2048,384]{1,0:T(8,128)(2,1)S(1)}, bf16[2048,384]{1,0:T(8,128)(2,1)}, u32[]{:S(2)}) copy-start(bf16[2048,384]{1,0:T(8,128)(2,1)} %weight_ref.1) | copy-start | bytes 4718596
  90.7 1.0 copy-start.7
  91.7 5.6 %copy-start.10 = (s32[128,2]{0,1:T(2,128)S(1)}, s32[128,2]{0,1:T(2,128)}, u32[]{:S(2)}) copy-start(s32[128,2]{0,1:T(2,128)} %param.19) | copy-start | bytes 3076
  91.9 5.9 %copy-start.9 = (f32[3072]{0:T(1024)S(1)}, f32[3072]{0:T(1024)}, u32[]{:S(2)}) copy-start(f32[3072]{0:T(1024)} %param.18) | copy-start | bytes 36868
  91.9 7.1 %copy-start.11 = (f32[128,2]{0,1:T(2,128)S(1)}, f32[128,2]{0,1:T(2,128)}, u32[]{:S(2)}) copy-start(f32[128,2]{0,1:T(2,128)} %param.20) | copy-start | bytes 3076
  92.9 6.6 %collective-permute-start = (bf16[128,3072]{1,0:T(8,128)(2,1)}, bf16[128,3072]{1,0:T(8,128)(2,1)S(1)}, u32[]{:S(2)}, u32[]{:S(2)}) collective-permute-start(bf16[128,3072]{1,0:T(8,128)(2,1)} %convert_element_type.81), channel_id=1, source_target_pairs={{0,1},{1,0},{2,3},{3,2},{4,5},{5,4},{6,7},{7,6},{8,9},{9,8},{10,11... | collective-permute-start | bytes 2359304 | tf_op jit(solution)/shard_map/ppermute | solution.py:22
  99.8 1.2 copy-start.3
  131.8 8.8 %copy-start.6 = (bf16[288,3072]{1,0:T(8,128)(2,1)S(1)}, bf16[288,3072]{1,0:T(8,128)(2,1)}, u32[]{:S(2)}) copy-start(bf16[288,3072]{1,0:T(8,128)(2,1)} %reshape.71) | copy-start | bytes 5308420
  131.8 18.4 %slice-start = ((s8[14155776]{0:T(1024)(128)(4,1)}), s8[4194304]{0:T(1024)(128)(4,1)S(1)}, s32[]{:S(2)}) async-start(s8[14155776]{0:T(1024)(128)(4,1)} %bitcast.71), calls=%async_computation | async-start | bytes 8388608
  131.8 18.4 %slice-start.1 = ((s8[14155776]{0:T(1024)(128)(4,1)}), s8[4194304]{0:T(1024)(128)(4,1)S(1)}, s32[]{:S(2)}) async-start(s8[14155776]{0:T(1024)(128)(4,1)} %bitcast.71), calls=%async_computation.1 | async-start | bytes 8388608
  140.6 9.6 %slice-start.2 = ((s8[14155776]{0:T(1024)(128)(4,1)}), s8[4194304]{0:T(1024)(128)(4,1)S(1)}, s32[]{:S(2)}) async-start(s8[14155776]{0:T(1024)(128)(4,1)} %bitcast.71), calls=%async_computation.2 | async-start | bytes 8388608
  140.6 9.6 %slice-start.3 = ((s8[14155776]{0:T(1024)(128)(4,1)}), s8[1572864]{0:T(1024)(128)(4,1)S(1)}, s32[]{:S(2)}) async-start(s8[14155776]{0:T(1024)(128)(4,1)} %bitcast.71), calls=%async_computation.3 | async-start | bytes 3145728
  185.1 1.4 copy-start.4
  185.1 2.5 %copy-start.1 = (bf16[128,2048]{1,0:T(8,128)(2,1)S(1)}, bf16[128,2048]{1,0:T(8,128)(2,1)}, u32[]{:S(2)}) copy-start(bf16[128,2048]{1,0:T(8,128)(2,1)} %param.13) | copy-start | bytes 1572868
